TPU v7x, 256 devices: a whole 4x4x8 slice. The times are simulated.
256 devices in a mesh: section: 4 (over y_hi, core), ctx: 16 (over y_lo, z), tp: 4 (over x).
Axes of the slice: x: 4, y: 4 (y_hi: 2, y_lo: 2; y = y_hi * 2 + y_lo), z: 8, core: 2. Of those that a mesh axis runs over, the one named last changes fastest.
Arguments:
- mixer_input: bfloat16 [4, 8192, 8192], P('section', 'ctx', 'tp'), may hold values from -6 to 6
- write_vectors: bfloat16 [4, 8192, 1024], P('section', 'ctx', 'tp'), may hold values from -6 to 6
- read_vectors: bfloat16 [4, 8192, 1024], P('section', 'ctx', 'tp'), may hold values from -6 to 6
- delta_raw: float32 [4, 8192, 128], P('section', 'ctx', 'tp'), as said below
- log_rates: float32 [4, 128], P('section', 'tp'), as said below
- delta_bias: float32 [4, 128], P('section', 'tp'), as said below
- skip_gain: float32 [4, 128], P('section', 'tp'), may hold values from 0.5 to 1.5
- output_grad: bfloat16 [4, 8192, 8192], P('section', 'ctx', 'tp'), may hold values from -6 to 6
Outputs:
- upstream_grad: bfloat16 [4, 8192, 8192], P('section', 'ctx', 'tp')
- grad_delta: float32 [4, 8192, 128], P('section', 'ctx', 'tp')
- grad_vectors: float32 [4, 8192, 2048], P('section', ('ctx', 'tp'))
- grad_params: float32 [4, 3, 128], P('section', None, 'tp')
Inputs may be any that keep to these rules, and one draw needn't show every extreme that they name: `log_rates`: one value a head and section. `delta_bias`: one value a head and section. `delta_raw`: real-valued logits.
All inputs are finite; a program needn't handle non-finite values.
Results may differ from a plain program's by a relative error of at most 0.00365.
Values may be sent and summed in bfloat16 or wider, within the bound.
No kernel may reach another device: no remote copies, remote signals or barrier semaphores. Data moves between devices by JAX's collectives and lax.ppermute only.
A program may use at most 128 MiB of HBM per device.

v0:
```python
import jax
import jax.numpy as jnp
from jax import lax
from jax.sharding import PartitionSpec as P

HEADDIM = 64
STATE = 128
BLOCK = 256


HIGHEST = lax.Precision.HIGHEST


def prefix(x, axis, combine, identity):
    devices, place = (lax.axis_size(axis), lax.axis_index(axis))
    everything = jax.tree.map(
        lambda part, kind: lax.all_gather(part.astype(kind), axis), x, (jnp.bfloat16, jnp.bfloat16)
    )
    start = jax.tree.map(
        lambda part, zero: jnp.broadcast_to(jnp.asarray(zero, part.dtype), part.shape), x, identity
    )

    def hop(k, before):
        reached = k < place
        new = combine(
            before, jax.tree.map(lambda part, own: part[k].astype(own.dtype), everything, x)
        )
        return jax.tree.map(lambda a, b: jnp.where(reached, a, b), new, before)

    return lax.fori_loop(0, devices, hop, start)


def shifted(block, axis, distance):
    devices = range(lax.axis_size(axis))
    route = [(i - distance, i) for i in devices if i - distance in devices]
    return lax.ppermute(block, axis, route)


def block_pass(values_all, write_rows, read_rows, step_size, decay_rates, start_state):
    length, group_count, per_group, head_width = values_all.shape
    block_count = length // BLOCK
    positions = jnp.arange(BLOCK)
    causal = positions[:, None] >= positions[None, :]

    def advance(carry_state, block_item):
        values, write_block, read_block, step_rows = block_item
        cum_log = jnp.cumsum(-step_rows * decay_rates[None], axis=0)
        gap_logs = cum_log[:, None] - cum_log[None, :]
        decay_mat = jnp.exp(jnp.where(causal[:, :, None, None], gap_logs, -1e30))
        scores = jnp.einsum("ign,jgn->ijg", read_block, write_block, precision=HIGHEST)
        weights = scores[:, :, :, None] * decay_mat * step_rows[None]
        within = jnp.einsum("ijgk,jgkp->igkp", weights, values, precision=HIGHEST)
        carried = jnp.einsum("ign,gkpn->igkp", read_block, carry_state, precision=HIGHEST)
        outputs = within + jnp.exp(cum_log)[..., None] * carried
        tail_w = jnp.exp(cum_log[-1][None] - cum_log) * step_rows
        written = jnp.einsum(
            "jgkp,jgn->gkpn", tail_w[..., None] * values, write_block, precision=HIGHEST
        )
        new_state = jnp.exp(cum_log[-1])[..., None, None] * carry_state + written
        return (new_state, outputs)

    blocks_in = (
        values_all.reshape(block_count, BLOCK, group_count, per_group, head_width),
        write_rows.reshape(block_count, BLOCK, group_count, -1),
        read_rows.reshape(block_count, BLOCK, group_count, -1),
        step_size.reshape(block_count, BLOCK, group_count, per_group),
    )
    last_state, outputs = lax.scan(jax.checkpoint(advance), start_state, blocks_in)
    return (outputs.reshape(length, group_count, per_group, head_width), last_state)


def decay_terms(delta_rows, rate_logs, bias_terms):
    step_size = jax.nn.softplus(delta_rows + bias_terms[None, :])
    decay_rates = jnp.exp(rate_logs)
    cum_log = jnp.cumsum(-step_size * decay_rates[None, :], axis=0)
    return (step_size, decay_rates, cum_log)


def layer_output(input_rows, write_rows, read_rows, delta_rows, rate_logs, bias_terms, skip_terms):
    length = input_rows.shape[0]
    group_count = write_rows.shape[1] // STATE
    head_count = rate_logs.shape[0]
    per_group = head_count // group_count
    step_size = jax.nn.softplus(delta_rows + bias_terms[None, :]).reshape(
        length, group_count, per_group
    )
    decay_rates = jnp.exp(rate_logs).reshape(group_count, per_group)
    values = input_rows.reshape(length, group_count, per_group, HEADDIM)
    start_state = jnp.zeros((group_count, per_group, HEADDIM, STATE), jnp.float32)
    outputs, unused = block_pass(
        values,
        write_rows.reshape(length, group_count, STATE),
        read_rows.reshape(length, group_count, STATE),
        step_size,
        decay_rates,
        start_state,
    )
    outputs = outputs + skip_terms.reshape(group_count, per_group)[None, :, :, None] * values
    return outputs.reshape(input_rows.shape)


def local_state(input_rows, write_rows, delta_rows, rate_logs, bias_terms):
    length = input_rows.shape[0]
    group_count = write_rows.shape[1] // STATE
    per_group = rate_logs.shape[0] // group_count
    step_size, decay_rates, cum_log = decay_terms(delta_rows, rate_logs, bias_terms)
    tail_w = (jnp.exp(cum_log[-1][None, :] - cum_log) * step_size).reshape(
        length, group_count, per_group
    )
    values = input_rows.reshape(length, group_count, per_group, HEADDIM)
    return jnp.einsum(
        "tgkp,tgn->gkpn",
        tail_w[..., None] * values,
        write_rows.reshape(length, group_count, STATE),
        precision=HIGHEST,
    )


def cross_terms(read_rows, delta_rows, rate_logs, bias_terms, entry_state):
    length = read_rows.shape[0]
    group_count = read_rows.shape[1] // STATE
    per_group = rate_logs.shape[0] // group_count
    step_size, decay_rates, cum_log = decay_terms(delta_rows, rate_logs, bias_terms)
    seen = jnp.einsum(
        "tgn,gkpn->tgkp",
        read_rows.reshape(length, group_count, STATE),
        entry_state,
        precision=HIGHEST,
    )
    scale_rows = jnp.exp(cum_log).reshape(length, group_count, per_group)
    outputs = (scale_rows[..., None] * seen).reshape(length, -1)
    ending = jnp.exp(cum_log[-1]).reshape(group_count, per_group)[..., None, None] * entry_state
    return (outputs, ending)


def link_blocks(earlier, later):
    return (earlier[0] + later[0], jnp.exp(later[0])[..., None, None] * earlier[1] + later[1])


def shards(
    mixer_input,
    write_vectors,
    read_vectors,
    delta_raw,
    log_rates,
    delta_bias,
    skip_gain,
    output_grad,
):
    input_rows = mixer_input[0].astype(jnp.float32)
    write_rows = write_vectors[0].astype(jnp.float32)
    read_rows = read_vectors[0].astype(jnp.float32)
    delta_rows = delta_raw[0]
    rate_logs = log_rates[0]
    bias_terms = delta_bias[0]
    skip_terms = skip_gain[0]
    grad_rows = output_grad[0].astype(jnp.float32)
    length = input_rows.shape[0]
    head_count = rate_logs.shape[0]
    group_count = write_rows.shape[1] // STATE
    per_group = head_count // group_count
    step_size, decay_rates, cum_log = decay_terms(delta_rows, rate_logs, bias_terms)
    total_grid = cum_log[-1].reshape(group_count, per_group)
    local_end, state_pull = jax.vjp(
        local_state, input_rows, write_rows, delta_rows, rate_logs, bias_terms
    )
    grad_values = grad_rows.reshape(length, group_count, per_group, HEADDIM)
    scale_rows = jnp.exp(cum_log).reshape(length, group_count, per_group)
    entry_grad = jnp.einsum(
        "tgkp,tgn->gkpn",
        scale_rows[..., None] * grad_values,
        read_rows.reshape(length, group_count, STATE),
        precision=HIGHEST,
    )
    identity = (jnp.zeros_like(total_grid), jnp.zeros_like(local_end))
    unused_log, entry_state = prefix((total_grid, local_end), "ctx", link_blocks, identity)
    own_decay = jnp.exp(total_grid)[..., None, None]

    def relay_turn(turn, running):
        sending = entry_grad + own_decay * running
        return shifted(sending, "ctx", -1)

    exit_grad = lax.fori_loop(0, lax.axis_size("ctx") - 1, relay_turn, jnp.zeros_like(entry_grad))

    def combined(input_in, write_in, read_in, delta_in, rates_in, bias_in, skip_in):
        direct = layer_output(input_in, write_in, read_in, delta_in, rates_in, bias_in, skip_in)
        ending = local_state(input_in, write_in, delta_in, rates_in, bias_in)
        seen_out, seen_end = cross_terms(read_in, delta_in, rates_in, bias_in, entry_state)
        return (direct + seen_out, ending + seen_end)

    unused_joint, joint_pull = jax.vjp(
        combined, input_rows, write_rows, read_rows, delta_rows, rate_logs, bias_terms, skip_terms
    )
    gradients = joint_pull((grad_rows, exit_grad))
    grad_input = gradients[0]
    grad_write = gradients[1]
    grad_read = gradients[2]
    grad_delta = gradients[3]
    grad_rate = gradients[4]
    grad_bias = gradients[5]
    grad_skip = gradients[6]
    upstream = shifted(grad_input.astype(jnp.bfloat16)[None], "section", -1)
    paired = jnp.stack(
        [
            grad_write.reshape(length, group_count, STATE),
            grad_read.reshape(length, group_count, STATE),
        ],
        axis=2,
    )
    paired = paired.reshape(length, group_count * 2 * STATE)[None]
    vector_rows = lax.all_to_all(paired, "tp", split_axis=1, concat_axis=2, tiled=True)
    param_sums = lax.psum(jnp.stack([grad_rate, grad_bias, grad_skip])[None], "ctx")
    return (upstream, grad_delta[None], vector_rows, param_sums)


def solution(mesh):
    in_specs = (
        P("section", "ctx", "tp"),
        P("section", "ctx", "tp"),
        P("section", "ctx", "tp"),
        P("section", "ctx", "tp"),
        P("section", "tp"),
        P("section", "tp"),
        P("section", "tp"),
        P("section", "ctx", "tp"),
    )
    out_specs = (
        P("section", "ctx", "tp"),
        P("section", "ctx", "tp"),
        P("section", ("ctx", "tp"), None),
        P("section", None, "tp"),
    )
    return jax.shard_map(shards, mesh=mesh, in_specs=in_specs, out_specs=out_specs, check_vma=False)
```

profile of v0, /device:TPU:50, one launch (start us, length us, event | category | flops | bytes accessed | tf_op | source)
XLA Modules:
  0.0 1008.6 jit_solution(6337760211798281752)
XLA Ops:
  51.8 446.3 %while.62 = (s32[]{:T(128)}, f32[2,16,64,128]{3,2,1,0:T(8,128)S(1)}, f32[2,16,1,1]{1,0,3,2:T(2,128)S(1)}, f32[2,16,64,128]{3,2,1,0:T(8,128)}, s32[]{:T(128)}) while((s32[]{:T(128)}, f32[2,16,64,128]{3,2,1,0:T(8,128)S(1)}, f32[2,16,1,1]{1,0,3,2:T(2,128)S(1)}, f32[2,16,64,128]{3,2,1,0:T(8,128)}, s32[]{:T(128)}) %tuple.170), condition=%wide.region_5.7_spmd, body=%wide.region_4.6_spmd.sunk | while | flops 524290 | bytes 7340261 | solution.py:183
  56.2 48.3 %collective-permute-done = f32[2,16,64,128]{3,2,1,0:T(8,128)S(1)} collective-permute-done((f32[2,16,64,128]{3,2,1,0:T(8,128)}, f32[2,16,64,128]{3,2,1,0:T(8,128)S(1)}, u32[]{:S(2)}, u32[]{:S(2)}) %collective-permute-start) | collective-permute-done | bytes 1048608 | tf_op jit(solution)/shard_map/while/body/eval_jaxpr/ppermute | solution.py:36
  108.9 48.1 %collective-permute-done = f32[2,16,64,128]{3,2,1,0:T(8,128)S(1)} collective-permute-done((f32[2,16,64,128]{3,2,1,0:T(8,128)}, f32[2,16,64,128]{3,2,1,0:T(8,128)S(1)}, u32[]{:S(2)}, u32[]{:S(2)}) %collective-permute-start) | collective-permute-done | bytes 1048608 | tf_op jit(solution)/shard_map/while/body/eval_jaxpr/ppermute | solution.py:36
  161.4 30.0 %collective-permute-done = f32[2,16,64,128]{3,2,1,0:T(8,128)S(1)} collective-permute-done((f32[2,16,64,128]{3,2,1,0:T(8,128)}, f32[2,16,64,128]{3,2,1,0:T(8,128)S(1)}, u32[]{:S(2)}, u32[]{:S(2)}) %collective-permute-start) | collective-permute-done | bytes 1048608 | tf_op jit(solution)/shard_map/while/body/eval_jaxpr/ppermute | solution.py:36
  196.1 24.3 %collective-permute-done = f32[2,16,64,128]{3,2,1,0:T(8,128)S(1)} collective-permute-done((f32[2,16,64,128]{3,2,1,0:T(8,128)}, f32[2,16,64,128]{3,2,1,0:T(8,128)S(1)}, u32[]{:S(2)}, u32[]{:S(2)}) %collective-permute-start) | collective-permute-done | bytes 1048608 | tf_op jit(solution)/shard_map/while/body/eval_jaxpr/ppermute | solution.py:36
  225.1 24.4 %collective-permute-done = f32[2,16,64,128]{3,2,1,0:T(8,128)S(1)} collective-permute-done((f32[2,16,64,128]{3,2,1,0:T(8,128)}, f32[2,16,64,128]{3,2,1,0:T(8,128)S(1)}, u32[]{:S(2)}, u32[]{:S(2)}) %collective-permute-start) | collective-permute-done | bytes 1048608 | tf_op jit(solution)/shard_map/while/body/eval_jaxpr/ppermute | solution.py:36
  253.8 24.2 %collective-permute-done = f32[2,16,64,128]{3,2,1,0:T(8,128)S(1)} collective-permute-done((f32[2,16,64,128]{3,2,1,0:T(8,128)}, f32[2,16,64,128]{3,2,1,0:T(8,128)S(1)}, u32[]{:S(2)}, u32[]{:S(2)}) %collective-permute-start) | collective-permute-done | bytes 1048608 | tf_op jit(solution)/shard_map/while/body/eval_jaxpr/ppermute | solution.py:36
  282.2 23.3 %collective-permute-done = f32[2,16,64,128]{3,2,1,0:T(8,128)S(1)} collective-permute-done((f32[2,16,64,128]{3,2,1,0:T(8,128)}, f32[2,16,64,128]{3,2,1,0:T(8,128)S(1)}, u32[]{:S(2)}, u32[]{:S(2)}) %collective-permute-start) | collective-permute-done | bytes 1048608 | tf_op jit(solution)/shard_map/while/body/eval_jaxpr/ppermute | solution.py:36
  309.8 22.5 %collective-permute-done = f32[2,16,64,128]{3,2,1,0:T(8,128)S(1)} collective-permute-done((f32[2,16,64,128]{3,2,1,0:T(8,128)}, f32[2,16,64,128]{3,2,1,0:T(8,128)S(1)}, u32[]{:S(2)}, u32[]{:S(2)}) %collective-permute-start) | collective-permute-done | bytes 1048608 | tf_op jit(solution)/shard_map/while/body/eval_jaxpr/ppermute | solution.py:36
  336.6 21.6 %collective-permute-done = f32[2,16,64,128]{3,2,1,0:T(8,128)S(1)} collective-permute-done((f32[2,16,64,128]{3,2,1,0:T(8,128)}, f32[2,16,64,128]{3,2,1,0:T(8,128)S(1)}, u32[]{:S(2)}, u32[]{:S(2)}) %collective-permute-start) | collective-permute-done | bytes 1048608 | tf_op jit(solution)/shard_map/while/body/eval_jaxpr/ppermute | solution.py:36
  362.4 20.7 %collective-permute-done = f32[2,16,64,128]{3,2,1,0:T(8,128)S(1)} collective-permute-done((f32[2,16,64,128]{3,2,1,0:T(8,128)}, f32[2,16,64,128]{3,2,1,0:T(8,128)S(1)}, u32[]{:S(2)}, u32[]{:S(2)}) %collective-permute-start) | collective-permute-done | bytes 1048608 | tf_op jit(solution)/shard_map/while/body/eval_jaxpr/ppermute | solution.py:36
  387.5 19.9 %collective-permute-done = f32[2,16,64,128]{3,2,1,0:T(8,128)S(1)} collective-permute-done((f32[2,16,64,128]{3,2,1,0:T(8,128)}, f32[2,16,64,128]{3,2,1,0:T(8,128)S(1)}, u32[]{:S(2)}, u32[]{:S(2)}) %collective-permute-start) | collective-permute-done | bytes 1048608 | tf_op jit(solution)/shard_map/while/body/eval_jaxpr/ppermute | solution.py:36
  411.6 19.0 %collective-permute-done = f32[2,16,64,128]{3,2,1,0:T(8,128)S(1)} collective-permute-done((f32[2,16,64,128]{3,2,1,0:T(8,128)}, f32[2,16,64,128]{3,2,1,0:T(8,128)S(1)}, u32[]{:S(2)}, u32[]{:S(2)}) %collective-permute-start) | collective-permute-done | bytes 1048608 | tf_op jit(solution)/shard_map/while/body/eval_jaxpr/ppermute | solution.py:36
  434.9 19.0 %collective-permute-done = f32[2,16,64,128]{3,2,1,0:T(8,128)S(1)} collective-permute-done((f32[2,16,64,128]{3,2,1,0:T(8,128)}, f32[2,16,64,128]{3,2,1,0:T(8,128)S(1)}, u32[]{:S(2)}, u32[]{:S(2)}) %collective-permute-start) | collective-permute-done | bytes 1048608 | tf_op jit(solution)/shard_map/while/body/eval_jaxpr/ppermute | solution.py:36
  458.3 19.0 %collective-permute-done = f32[2,16,64,128]{3,2,1,0:T(8,128)S(1)} collective-permute-done((f32[2,16,64,128]{3,2,1,0:T(8,128)}, f32[2,16,64,128]{3,2,1,0:T(8,128)S(1)}, u32[]{:S(2)}, u32[]{:S(2)}) %collective-permute-start) | collective-permute-done | bytes 1048608 | tf_op jit(solution)/shard_map/while/body/eval_jaxpr/ppermute | solution.py:36
  481.6 16.5 %collective-permute-done = f32[2,16,64,128]{3,2,1,0:T(8,128)S(1)} collective-permute-done((f32[2,16,64,128]{3,2,1,0:T(8,128)}, f32[2,16,64,128]{3,2,1,0:T(8,128)S(1)}, u32[]{:S(2)}, u32[]{:S(2)}) %collective-permute-start) | collective-permute-done | bytes 1048608 | tf_op jit(solution)/shard_map/while/body/eval_jaxpr/ppermute | solution.py:36
  513.4 30.5 %all_gather.10 = bf16[16,2,16]{2,1,0:T(2,128)(2,1)S(1)} all-gather(bf16[1,2,16]{2,1,0:T(2,128)(2,1)S(1)} %copy-done.56), channel_id=1, replica_groups=mesh['section'=4,'ctx'=16,'tp'=4] {'ctx'}, dimensions={0}, use_global_device_ids=true | all-gather | bytes 1088 | tf_op jit(solution)/shard_map/all_gather | solution.py:17
  543.8 21.4 %while.65 = (s32[]{:T(128)}, f32[2,16,64,128]{3,2,1,0:T(8,128)S(1)}, s32[]{:T(128)}, bf16[16,2,16]{2,1,0:T(2,128)(2,1)S(1)}, bf16[16,2,16,64,128]{4,3,2,1,0:T(8,128)(2,1)}, /*index=5*/s32[]{:T(128)}, s32[]{:T(128)}) while((s32[]{:T(128)}, f32[2,16,64,128]{3,2,1,0:T(8,128)S(1)}, s32[]{:T(128)}, ...), condition=%wide.region_26.28_spmd.clone, body=%wide.region_25.27_spmd.clone.sunk | while | flops 1310756 | bytes 2621865 | solution.py:30
  598.4 323.6 %while.64 = (s32[]{:T(128)}, f32[2,16]{1,0:T(2,128)}, f32[2,16,64,128]{3,2,1,0:T(8,128)}, f32[2,256,2,16,64]{1,0,4,3,2:T(2,128)}, f32[2,256,2,128]{1,0,3,2:T(2,1...) while((s32[]{:T(128)}, f32[2,16]{1,0:T(2,128)}, ...), condition=%wide.region_24.26_spmd.clone, body=%wide.region_10.25_spmd.clone.sunk | while | flops 7895728128 | bytes 109226232 | solution.py:68
  656.9 14.6 %fusion.194 = (f32[256,2,16]{0,2,1:T(8,128)}, f32[256,2,16]{0,2,1:T(8,128)}, f32[256,2,16]{0,2,1:T(8,128)}, f32[256,256,2]{1,0,2:T(8,128)S(1)}) fusion(f32[256,2,16]{0,2,1:T(8,128)S(1)} %copy.537, f32[256,2,16]{0,2,1:T(8,128)} %copy.538, f32[256,256,2]{1,0,2:T(8,128)} %copy.539, pred[256,256]{1,0:T(8,128)(4,1)} %iota_compare_fusion.2, ...), kind=kOutput, calls=%fused_computation.11.clone.1 | convolution fusion | flops 1637720064 | bytes 5472256 | tf_op jit(solution)/shard_map/transpose(jvp())/while/body/eval_jaxpr/checkpoint/ijgk,jgkp->igkp/dot_general | solution.py:52
  707.8 42.8 %dynamic_update_slice.57 = f32[2,256,2,16,64]{1,0,4,3,2:T(2,128)} dynamic-update-slice(f32[2,256,2,16,64]{1,0,4,3,2:T(2,128)} %get-tuple-element.1176, f32[1,256,2,16,64]{1,0,4,3,2:T(1,128)} %copy.551, s32[]{:T(128)S(6)} %sub.212, s32[]{:T(128)} %constant.144.clone.1..sunk.1, s32[]{:T(128)} %constant.144.clone.1..sunk.1, s32[]{:T(128)} %constant.144.clone.1..sunk.1, s32[]{:T(128)} %constant.144.clone.1..sunk.1) | dynamic-update-slice | bytes 4194308 | tf_op jit(solution)/shard_map/transpose(jvp())/while/body/jit(dynamic_update_index_in_dim)/dynamic_update_slice | solution.py:68
  804.4 14.6 %fusion.194 = (f32[256,2,16]{0,2,1:T(8,128)}, f32[256,2,16]{0,2,1:T(8,128)}, f32[256,2,16]{0,2,1:T(8,128)}, f32[256,256,2]{1,0,2:T(8,128)S(1)}) fusion(f32[256,2,16]{0,2,1:T(8,128)S(1)} %copy.537, f32[256,2,16]{0,2,1:T(8,128)} %copy.538, f32[256,256,2]{1,0,2:T(8,128)} %copy.539, pred[256,256]{1,0:T(8,128)(4,1)} %iota_compare_fusion.2, ...), kind=kOutput, calls=%fused_computation.11.clone.1 | convolution fusion | flops 1637720064 | bytes 5472256 | tf_op jit(solution)/shard_map/transpose(jvp())/while/body/eval_jaxpr/checkpoint/ijgk,jgkp->igkp/dot_general | solution.py:52
  855.4 42.8 %dynamic_update_slice.57 = f32[2,256,2,16,64]{1,0,4,3,2:T(2,128)} dynamic-update-slice(f32[2,256,2,16,64]{1,0,4,3,2:T(2,128)} %get-tuple-element.1176, f32[1,256,2,16,64]{1,0,4,3,2:T(1,128)} %copy.551, s32[]{:T(128)S(6)} %sub.212, s32[]{:T(128)} %constant.144.clone.1..sunk.1, s32[]{:T(128)} %constant.144.clone.1..sunk.1, s32[]{:T(128)} %constant.144.clone.1..sunk.1, s32[]{:T(128)} %constant.144.clone.1..sunk.1) | dynamic-update-slice | bytes 4194308 | tf_op jit(solution)/shard_map/transpose(jvp())/while/body/jit(dynamic_update_index_in_dim)/dynamic_update_slice | solution.py:68
  961.1 33.5 %psum.7 = f32[1,3,32]{2,1,0:T(4,128)S(1)} all-reduce(f32[1,3,32]{2,1,0:T(4,128)S(1)} %maximum_bitcast_fusion), channel_id=1, replica_groups=mesh['section'=4,'ctx'=16,'tp'=4] {'ctx'}, use_global_device_ids=true, to_apply=%region_42.44 | all-reduce | flops 96 | bytes 768 | tf_op jit(solution)/shard_map/psum | solution.py:212
  (476 shorter events, 416.3 us)
Async XLA Ops:
  7.2 536.7 %all-gather.3.cloned.1.call-start = ((), (), s32[]{:S(2)}) async-start(), calls=%async_computation.1 | async-start | bytes 8912896 | tf_op jit(solution)/shard_map/all_gather | solution.py:17
  8.2 568.4 %copy-start.18 = (f32[1,512,32]{2,1,0:T(8,128)}, f32[1,512,32]{2,1,0:T(8,128)S(1)}, u32[]{:S(2)}) copy-start(f32[1,512,32]{2,1,0:T(8,128)S(1)} %copy.353) | copy-start | bytes 196612
  8.9 21.2 %copy-start.51 = (f32[32]{0:T(128)}, f32[32]{0:T(128)S(1)}, u32[]{:S(2)}) copy-start(f32[32]{0:T(128)S(1)} %get-tuple-element.849) | copy-start | bytes 388
  13.2 484.9 %copy-start.31 = (f32[512,32]{0,1:T(8,128)}, f32[512,32]{0,1:T(8,128)S(1)}, u32[]{:S(2)}) copy-start(f32[512,32]{0,1:T(8,128)S(1)} %copy.357) | copy-start | bytes 196612
  54.1 50.3 %collective-permute-start = (f32[2,16,64,128]{3,2,1,0:T(8,128)}, f32[2,16,64,128]{3,2,1,0:T(8,128)S(1)}, u32[]{:S(2)}, u32[]{:S(2)}) collective-permute-start(f32[2,16,64,128]{3,2,1,0:T(8,128)} %multiply_add_fusion.3), channel_id=1, source_target_pairs={{4,0},{8,4},{12,8},{16,12},{20,16},{24,20},{28,24},{32,28},{36,32}... | collective-permute-start | bytes 3145736 | tf_op jit(solution)/shard_map/while/body/eval_jaxpr/ppermute | solution.py:36
  106.8 50.1 %collective-permute-start = (f32[2,16,64,128]{3,2,1,0:T(8,128)}, f32[2,16,64,128]{3,2,1,0:T(8,128)S(1)}, u32[]{:S(2)}, u32[]{:S(2)}) collective-permute-start(f32[2,16,64,128]{3,2,1,0:T(8,128)} %multiply_add_fusion.3), channel_id=1, source_target_pairs={{4,0},{8,4},{12,8},{16,12},{20,16},{24,20},{28,24},{32,28},{36,32}... | collective-permute-start | bytes 3145736 | tf_op jit(solution)/shard_map/while/body/eval_jaxpr/ppermute | solution.py:36
  159.3 32.0 %collective-permute-start = (f32[2,16,64,128]{3,2,1,0:T(8,128)}, f32[2,16,64,128]{3,2,1,0:T(8,128)S(1)}, u32[]{:S(2)}, u32[]{:S(2)}) collective-permute-start(f32[2,16,64,128]{3,2,1,0:T(8,128)} %multiply_add_fusion.3), channel_id=1, source_target_pairs={{4,0},{8,4},{12,8},{16,12},{20,16},{24,20},{28,24},{32,28},{36,32}... | collective-permute-start | bytes 3145736 | tf_op jit(solution)/shard_map/while/body/eval_jaxpr/ppermute | solution.py:36
  193.7 26.7 %collective-permute-start = (f32[2,16,64,128]{3,2,1,0:T(8,128)}, f32[2,16,64,128]{3,2,1,0:T(8,128)S(1)}, u32[]{:S(2)}, u32[]{:S(2)}) collective-permute-start(f32[2,16,64,128]{3,2,1,0:T(8,128)} %multiply_add_fusion.3), channel_id=1, source_target_pairs={{4,0},{8,4},{12,8},{16,12},{20,16},{24,20},{28,24},{32,28},{36,32}... | collective-permute-start | bytes 3145736 | tf_op jit(solution)/shard_map/while/body/eval_jaxpr/ppermute | solution.py:36
  222.8 26.8 %collective-permute-start = (f32[2,16,64,128]{3,2,1,0:T(8,128)}, f32[2,16,64,128]{3,2,1,0:T(8,128)S(1)}, u32[]{:S(2)}, u32[]{:S(2)}) collective-permute-start(f32[2,16,64,128]{3,2,1,0:T(8,128)} %multiply_add_fusion.3), channel_id=1, source_target_pairs={{4,0},{8,4},{12,8},{16,12},{20,16},{24,20},{28,24},{32,28},{36,32}... | collective-permute-start | bytes 3145736 | tf_op jit(solution)/shard_map/while/body/eval_jaxpr/ppermute | solution.py:36
  251.9 26.1 %collective-permute-start = (f32[2,16,64,128]{3,2,1,0:T(8,128)}, f32[2,16,64,128]{3,2,1,0:T(8,128)S(1)}, u32[]{:S(2)}, u32[]{:S(2)}) collective-permute-start(f32[2,16,64,128]{3,2,1,0:T(8,128)} %multiply_add_fusion.3), channel_id=1, source_target_pairs={{4,0},{8,4},{12,8},{16,12},{20,16},{24,20},{28,24},{32,28},{36,32}... | collective-permute-start | bytes 3145736 | tf_op jit(solution)/shard_map/while/body/eval_jaxpr/ppermute | solution.py:36
  280.3 25.2 %collective-permute-start = (f32[2,16,64,128]{3,2,1,0:T(8,128)}, f32[2,16,64,128]{3,2,1,0:T(8,128)S(1)}, u32[]{:S(2)}, u32[]{:S(2)}) collective-permute-start(f32[2,16,64,128]{3,2,1,0:T(8,128)} %multiply_add_fusion.3), channel_id=1, source_target_pairs={{4,0},{8,4},{12,8},{16,12},{20,16},{24,20},{28,24},{32,28},{36,32}... | collective-permute-start | bytes 3145736 | tf_op jit(solution)/shard_map/while/body/eval_jaxpr/ppermute | solution.py:36
  307.9 24.4 %collective-permute-start = (f32[2,16,64,128]{3,2,1,0:T(8,128)}, f32[2,16,64,128]{3,2,1,0:T(8,128)S(1)}, u32[]{:S(2)}, u32[]{:S(2)}) collective-permute-start(f32[2,16,64,128]{3,2,1,0:T(8,128)} %multiply_add_fusion.3), channel_id=1, source_target_pairs={{4,0},{8,4},{12,8},{16,12},{20,16},{24,20},{28,24},{32,28},{36,32}... | collective-permute-start | bytes 3145736 | tf_op jit(solution)/shard_map/while/body/eval_jaxpr/ppermute | solution.py:36
  334.6 23.5 %collective-permute-start = (f32[2,16,64,128]{3,2,1,0:T(8,128)}, f32[2,16,64,128]{3,2,1,0:T(8,128)S(1)}, u32[]{:S(2)}, u32[]{:S(2)}) collective-permute-start(f32[2,16,64,128]{3,2,1,0:T(8,128)} %multiply_add_fusion.3), channel_id=1, source_target_pairs={{4,0},{8,4},{12,8},{16,12},{20,16},{24,20},{28,24},{32,28},{36,32}... | collective-permute-start | bytes 3145736 | tf_op jit(solution)/shard_map/while/body/eval_jaxpr/ppermute | solution.py:36
  360.5 22.7 %collective-permute-start = (f32[2,16,64,128]{3,2,1,0:T(8,128)}, f32[2,16,64,128]{3,2,1,0:T(8,128)S(1)}, u32[]{:S(2)}, u32[]{:S(2)}) collective-permute-start(f32[2,16,64,128]{3,2,1,0:T(8,128)} %multiply_add_fusion.3), channel_id=1, source_target_pairs={{4,0},{8,4},{12,8},{16,12},{20,16},{24,20},{28,24},{32,28},{36,32}... | collective-permute-start | bytes 3145736 | tf_op jit(solution)/shard_map/while/body/eval_jaxpr/ppermute | solution.py:36
  385.5 21.8 %collective-permute-start = (f32[2,16,64,128]{3,2,1,0:T(8,128)}, f32[2,16,64,128]{3,2,1,0:T(8,128)S(1)}, u32[]{:S(2)}, u32[]{:S(2)}) collective-permute-start(f32[2,16,64,128]{3,2,1,0:T(8,128)} %multiply_add_fusion.3), channel_id=1, source_target_pairs={{4,0},{8,4},{12,8},{16,12},{20,16},{24,20},{28,24},{32,28},{36,32}... | collective-permute-start | bytes 3145736 | tf_op jit(solution)/shard_map/while/body/eval_jaxpr/ppermute | solution.py:36
  409.7 21.0 %collective-permute-start = (f32[2,16,64,128]{3,2,1,0:T(8,128)}, f32[2,16,64,128]{3,2,1,0:T(8,128)S(1)}, u32[]{:S(2)}, u32[]{:S(2)}) collective-permute-start(f32[2,16,64,128]{3,2,1,0:T(8,128)} %multiply_add_fusion.3), channel_id=1, source_target_pairs={{4,0},{8,4},{12,8},{16,12},{20,16},{24,20},{28,24},{32,28},{36,32}... | collective-permute-start | bytes 3145736 | tf_op jit(solution)/shard_map/while/body/eval_jaxpr/ppermute | solution.py:36
  433.0 21.0 %collective-permute-start = (f32[2,16,64,128]{3,2,1,0:T(8,128)}, f32[2,16,64,128]{3,2,1,0:T(8,128)S(1)}, u32[]{:S(2)}, u32[]{:S(2)}) collective-permute-start(f32[2,16,64,128]{3,2,1,0:T(8,128)} %multiply_add_fusion.3), channel_id=1, source_target_pairs={{4,0},{8,4},{12,8},{16,12},{20,16},{24,20},{28,24},{32,28},{36,32}... | collective-permute-start | bytes 3145736 | tf_op jit(solution)/shard_map/while/body/eval_jaxpr/ppermute | solution.py:36
  456.3 21.0 %collective-permute-start = (f32[2,16,64,128]{3,2,1,0:T(8,128)}, f32[2,16,64,128]{3,2,1,0:T(8,128)S(1)}, u32[]{:S(2)}, u32[]{:S(2)}) collective-permute-start(f32[2,16,64,128]{3,2,1,0:T(8,128)} %multiply_add_fusion.3), channel_id=1, source_target_pairs={{4,0},{8,4},{12,8},{16,12},{20,16},{24,20},{28,24},{32,28},{36,32}... | collective-permute-start | bytes 3145736 | tf_op jit(solution)/shard_map/while/body/eval_jaxpr/ppermute | solution.py:36
  479.7 18.4 %collective-permute-start = (f32[2,16,64,128]{3,2,1,0:T(8,128)}, f32[2,16,64,128]{3,2,1,0:T(8,128)S(1)}, u32[]{:S(2)}, u32[]{:S(2)}) collective-permute-start(f32[2,16,64,128]{3,2,1,0:T(8,128)} %multiply_add_fusion.3), channel_id=1, source_target_pairs={{4,0},{8,4},{12,8},{16,12},{20,16},{24,20},{28,24},{32,28},{36,32}... | collective-permute-start | bytes 3145736 | tf_op jit(solution)/shard_map/while/body/eval_jaxpr/ppermute | solution.py:36
  498.1 67.2 %copy-start.5 = (f32[2,16,64,128]{3,2,1,0:T(8,128)}, f32[2,16,64,128]{3,2,1,0:T(8,128)S(1)}, u32[]{:S(2)}) copy-start(f32[2,16,64,128]{3,2,1,0:T(8,128)S(1)} %get-tuple-element.466) | copy-start | bytes 3145732
  928.6 16.1 %copy-start.6 = (f32[2,16,64,128]{3,2,1,0:T(8,128)S(1)}, f32[2,16,64,128]{3,2,1,0:T(8,128)}, u32[]{:S(2)}) copy-start(f32[2,16,64,128]{3,2,1,0:T(8,128)} %copy-done.5) | copy-start | bytes 3145732
  928.6 16.1 %copy-start.32 = (f32[512,32]{0,1:T(8,128)S(1)}, f32[512,32]{0,1:T(8,128)}, u32[]{:S(2)}) copy-start(f32[512,32]{0,1:T(8,128)} %copy-done.31) | copy-start | bytes 196612
  934.5 63.2 %collective-permute-start.1 = (bf16[1,512,2048]{1,2,0:T(8,128)(2,1)}, bf16[1,512,2048]{1,2,0:T(8,128)(2,1)}, u32[]{:S(2)}, u32[]{:S(2)}) collective-permute-start(bf16[1,512,2048]{1,2,0:T(8,128)(2,1)} %get-tuple-element.840), channel_id=1, source_target_pairs={{64,0},{128,64},{192,128},{65,1},{129,65},{193,129},{66,2},{130,66... | collective-permute-start | bytes 6291464 | tf_op jit(solution)/shard_map/ppermute | solution.py:36
  954.9 41.1 %all-to-all-start = ((f32[1,512,512]{2,0,1:T(1,128)}), f32[1,512,512]{2,0,1:T(1,128)S(1)}, u32[]{:S(2)}, u32[]{:S(2)}) async-start(f32[1,512,512]{2,0,1:T(1,128)} %copy.395), calls=%async_computation | async-start | bytes 2097152 | tf_op jit(solution)/shard_map/all_to_all | solution.py:211
  (70 other events, 442.9 us)
Sparse Core Ops, SparseCore 0:
  24.2 149.9 all-gather.2
where the time goes:
time: 1030 us; the launch traced here: 1010 us
  waiting for transfers between devices  381 us (37%)
  local copies, waits for them, and re-layouts  228 us (22%)
  matrix products  134 us (13%)
  other arithmetic  119 us (12%)
  blocking collectives  64 us (6%)
  starting transfers between devices  36.7 us (4%)
  loops' own time  31.1 us (3%)
  between operations  14.9 us (1%)
    ppermute x16, waiting for transfers between devices, shifted(): return lax.ppermute(block, axis, route)  381 us
    dynamic_update_slice x14, local copies, waits for them, and re-layouts, block_pass(): lax.scan(jax.checkpoint(advance), start_state, blocks_in)  124 us
    dot_general x4, matrix products, advance(): within = jnp.einsum('ijgk,jgkp->igkp', weights, values, precision=HIGHEST)  47.2 us
    add x15, other arithmetic, relay_turn(): sending = entry_grad + own_decay * running  35.4 us
    psum x1, blocking collectives, shards(): lax.psum(jnp.stack([grad_rate, grad_bias, grad_skip])[None], 'ctx')  33.5 us
    ppermute x16, starting transfers between devices, shifted(): return lax.ppermute(block, axis, route)  31.8 us
    all_gather x1, blocking collectives, prefix(): lax.all_gather(part.astype(kind), axis)  30.5 us
    another operation x2, loops' own time, block_pass(): lax.scan(jax.checkpoint(advance), start_state, blocks_in)  30.4 us
  transfers between devices with their start and end apart: 18, of which 15 were waited for; matrix products, arithmetic and copies ran while one was open for 10% of the time, Pallas kernels for 0%

commit v1 on v0

v1 whole, which is shorter than its diff:
```python
import functools

import jax
import jax.numpy as jnp
from jax import lax
from jax.experimental import pallas as pl
from jax.experimental.pallas import tpu as pltpu
from jax.sharding import PartitionSpec as P

HEADDIM = 64
STATE = 128
CHUNK = 128
LANES = 128
F32 = jnp.float32
BF16 = jnp.bfloat16
TAIL = 16


def iota(shape, dim):
    return lax.broadcasted_iota(jnp.int32, shape, dim)


def mm(a, b):
    return lax.dot_general(a, b, (((1,), (0,)), ((), ())), preferred_element_type=F32)


def mm_nt(a, b):
    return lax.dot_general(a, b, (((1,), (1,)), ((), ())), preferred_element_type=F32)


def split2(v):
    hi = v.astype(BF16)
    return hi, (v - hi.astype(F32)).astype(BF16)


def split3(v):
    hi = v.astype(BF16)
    rest = v - hi.astype(F32)
    mid = rest.astype(BF16)
    return hi, mid, (rest - mid.astype(F32)).astype(BF16)


def softplus(z):
    u = jnp.exp(-jnp.abs(z))
    small = u * (1.0 - u * (0.5 - u * (1.0 / 3.0 - u * (0.25 - u * 0.2))))
    return jnp.maximum(z, 0.0) + jnp.where(u < 0.03, small, jnp.log(1.0 + u))


def chunk_rows(c):
    return slice(c * CHUNK, (c + 1) * CHUNK)


def expand(split, pair, heads):
    depth = split.shape[1]
    row, col = iota((depth, 2 * LANES), 0), iota((depth, 2 * LANES), 1)
    kind = (row % (2 * heads)) // heads
    head = row % heads
    hit = (kind == col // LANES) & (head == 2 * pair + (col % LANES) // HEADDIM)
    out = mm(split, jnp.where(hit, 1.0, 0.0).astype(BF16))
    return out[:, :LANES], out[:, LANES:]


def head_sum(product, pair, offset):
    hi, lo = split2(product)
    row, col = iota((2 * LANES, LANES), 0), iota((2 * LANES, LANES), 1)
    hit = col == offset + 2 * pair + (row % LANES) // HEADDIM
    return mm(jnp.concatenate([hi, lo], axis=1), jnp.where(hit, 1.0, 0.0).astype(BF16))


def prep_kernel(
    x_ref, dy_ref, w_ref, r_ref, delta_ref, rate_ref, bias_ref, pay_ref, cs_ref, ct_ref, wt_ref, rt_ref,
    *, per_group
):
    pair = pl.program_id(0)
    length = x_ref.shape[0]
    heads = delta_ref.shape[1]
    chunks = length // CHUNK

    @pl.when(pair == 0)
    def _():
        step = softplus(delta_ref[...] + bias_ref[...])
        logs = jnp.maximum(jnp.log(step), -200.0)
        decay = -step * jnp.exp(rate_ref[...])
        lower = jnp.where(iota((CHUNK, CHUNK), 0) >= iota((CHUNK, CHUNK), 1), 1.0, 0.0).astype(BF16)
        for c in range(chunks):
            hi, mid, lo = split3(decay[chunk_rows(c)])
            cum = mm(lower, hi) + mm(lower, mid) + mm(lower, lo)
            both = jnp.concatenate([cum, cum - logs[chunk_rows(c)]], axis=1)
            cs_ref[chunk_rows(c), :] = jnp.concatenate(split3(both), axis=1)
            ct_ref[c] = both.T

    @pl.when(pair % per_group == 0)
    def _():
        wt_ref[...] = w_ref[...].astype(F32).T.astype(BF16)
        rt_ref[...] = r_ref[...].astype(F32).T.astype(BF16)

    cl, ll = expand(cs_ref[...], pair, heads)
    state = jnp.zeros((STATE, LANES), F32)
    total = jnp.zeros((1, LANES), F32)
    for c in range(chunks):
        rows = chunk_rows(c)
        end = cl[(c + 1) * CHUNK - 1 : (c + 1) * CHUNK]
        hi, lo = split2(x_ref[rows].astype(F32) * jnp.exp(end - ll[rows]))
        w_t = wt_ref[:, rows]
        state = jnp.exp(end) * state + mm(jnp.concatenate([w_t, w_t], 1), jnp.concatenate([hi, lo], 0))
        total = total + end
    grad = jnp.zeros((STATE, LANES), F32)
    for c in reversed(range(chunks)):
        rows = chunk_rows(c)
        end = cl[(c + 1) * CHUNK - 1 : (c + 1) * CHUNK]
        hi, lo = split2(dy_ref[rows].astype(F32) * jnp.exp(cl[rows]))
        r_t = rt_ref[:, rows]
        grad = jnp.exp(end) * grad + mm(jnp.concatenate([r_t, r_t], 1), jnp.concatenate([hi, lo], 0))
    pay_ref[0, :STATE] = state.astype(BF16)
    pay_ref[0, STATE : 2 * STATE] = grad.astype(BF16)
    carry = jnp.exp(total)
    carry_hi = carry.astype(BF16).astype(F32)
    picked = jnp.where(iota((TAIL, LANES), 0) == 0, carry_hi, carry - carry_hi)
    pay_ref[0, 2 * STATE :] = picked.astype(BF16)


def scan_kernel(in_ref, out_ref):
    places = in_ref.shape[0]

    def carry(c):
        tail = in_ref[c, 2 * STATE :].astype(F32)
        return tail[0:1] + tail[1:2]

    state = jnp.zeros((STATE, LANES), F32)
    for c in range(places):
        out_ref[c, :STATE] = state.astype(BF16)
        state = carry(c) * state + in_ref[c, :STATE].astype(F32)
    grad = jnp.zeros((STATE, LANES), F32)
    for c in reversed(range(places)):
        out_ref[c, STATE:] = grad.astype(BF16)
        grad = carry(c) * grad + in_ref[c, STATE : 2 * STATE].astype(F32)


def intra_kernel(
    x_ref, dy_ref, w_ref, r_ref, cs_ref, ct_ref, skip_ref, dxi_ref, vp_ref, dwr_ref, gsk_ref,
    sc_ref, sct_ref, dsc_ref, *, first_pair, heads
):
    place = pl.program_id(0)
    pair = first_pair + place
    length = x_ref.shape[0]
    chunks = length // CHUNK

    @pl.when(place == 0)
    def _():
        for c in range(chunks):
            rows = chunk_rows(c)
            sc_ref[c] = mm_nt(r_ref[rows], w_ref[rows])
            sct_ref[c] = mm_nt(w_ref[rows], r_ref[rows])
        dsc_ref[...] = jnp.zeros_like(dsc_ref)
        vp_ref[...] = jnp.zeros_like(vp_ref)

    cl, ll = expand(cs_ref[...], pair, heads)
    row, col = iota((CHUNK, CHUNK), 0), iota((CHUNK, CHUNK), 1)
    left = iota((CHUNK, LANES), 1) < HEADDIM
    left_b = jnp.where(left, 1.0, 0.0).astype(BF16)
    right_b = jnp.where(left, 0.0, 1.0).astype(BF16)
    skip_sum = jnp.zeros((1, LANES), F32)
    for c in range(chunks):
        rows = chunk_rows(c)
        x, dy = x_ref[rows], dy_ref[rows]
        x_two = jnp.concatenate([x * left_b, x * right_b], axis=0)
        dy_two = jnp.concatenate([dy * left_b, dy * right_b], axis=0)
        gram = mm_nt(dy, x_two)
        mixes, mixes_t = [], []
        total = dsc_ref[c]
        for k in range(2):
            lane = slice(k * HEADDIM, k * HEADDIM + 1)
            log_row = ct_ref[c, pl.ds(heads + 2 * pair + k, 1), :]
            gap = jnp.where(row >= col, cl[rows, lane] - log_row, -1e30)
            decay = jnp.exp(gap)
            mixes.append((sc_ref[c] * decay).astype(BF16))
            total = total + gram[:, k * CHUNK : (k + 1) * CHUNK] * decay
            cum_row = ct_ref[c, pl.ds(2 * pair + k, 1), :]
            gap_t = jnp.where(col >= row, cum_row - ll[rows, lane], -1e30)
            mixes_t.append((sct_ref[c] * jnp.exp(gap_t)).astype(BF16))
        dsc_ref[c] = total
        y = mm(jnp.concatenate(mixes, axis=1), x_two)
        dx = mm(jnp.concatenate(mixes_t, axis=1), dy_two)
        xf, dyf = x.astype(F32), dy.astype(F32)
        pulled = xf * dx
        vp_ref[rows] += head_sum(dyf * y - pulled, pair, 0) + head_sum(pulled, pair, 2 * heads)
        dxi_ref[rows] = dx + skip_ref[...] * dyf
        skip_sum = skip_sum + jnp.sum(xf * dyf, axis=0, keepdims=True)
    gsk_ref[pl.ds(place, 1), :] = skip_sum

    @pl.when(place == pl.num_programs(0) - 1)
    def _():
        for c in range(chunks):
            rows = chunk_rows(c)
            w, r = w_ref[rows], r_ref[rows]
            total = dsc_ref[c]
            hi, lo = split2(total)
            dwr_ref[rows, STATE:] = mm(jnp.concatenate([hi, lo], 1), jnp.concatenate([w, w], 0))
            hi, lo = split2(total.T)
            dwr_ref[rows, :STATE] = mm(jnp.concatenate([hi, lo], 1), jnp.concatenate([r, r], 0))


def inter_kernel(
    x_ref, dy_ref, w_ref, r_ref, wt_ref, rt_ref, cs_ref, st_ref, dxi_ref, vp_in_ref, dwr_in_ref,
    up_ref, vp_ref, dwr_ref, states_ref, *, first_pair, heads
):
    place = pl.program_id(0)
    pair = first_pair + place
    length = x_ref.shape[0]
    chunks = length // CHUNK

    @pl.when(place == 0)
    def _():
        vp_ref[...] = vp_in_ref[...]
        dwr_ref[...] = dwr_in_ref[...]

    cl, ll = expand(cs_ref[...], pair, heads)
    last = iota((CHUNK, LANES), 0) == CHUNK - 1
    state = st_ref[0, :STATE].astype(F32)
    for c in range(chunks):
        rows = chunk_rows(c)
        states_ref[c] = state
        end = cl[(c + 1) * CHUNK - 1 : (c + 1) * CHUNK]
        tail = jnp.exp(end - ll[rows])
        hi, lo = split2(x_ref[rows].astype(F32) * tail)
        w_t = wt_ref[:, rows]
        state = jnp.exp(end) * state + mm(jnp.concatenate([w_t, w_t], 1), jnp.concatenate([hi, lo], 0))
    states_ref[chunks] = state
    grad = st_ref[0, STATE:].astype(F32)
    for c in reversed(range(chunks)):
        rows = chunk_rows(c)
        end = cl[(c + 1) * CHUNK - 1 : (c + 1) * CHUNK]
        w, r = w_ref[rows], r_ref[rows]
        xf, dyf = x_ref[rows].astype(F32), dy_ref[rows].astype(F32)
        tail = jnp.exp(end - ll[rows])
        seen = jnp.exp(cl[rows])
        s_hi, s_lo = split2(states_ref[c])
        g_hi, g_lo = split2(grad)
        y = seen * mm(jnp.concatenate([r, r], 1), jnp.concatenate([s_hi, s_lo], 0))
        dx = tail * mm(jnp.concatenate([w, w], 1), jnp.concatenate([g_hi, g_lo], 0))
        edge = jnp.sum(states_ref[c + 1] * grad, axis=0, keepdims=True)
        pulled = xf * dx
        push = dyf * y - pulled + jnp.where(last, edge, 0.0)
        vp_ref[rows] += head_sum(push, pair, 0) + head_sum(pulled, pair, 2 * heads)
        up_ref[rows] = (dxi_ref[rows] + dx).astype(BF16)
        d_hi, d_lo = split2(dyf * seen)
        x_hi, x_lo = split2(xf * tail)
        dwr_ref[rows, :STATE] += mm_nt(
            jnp.concatenate([x_hi, x_lo, x_hi], 1), jnp.concatenate([g_hi, g_hi, g_lo], 1)
        )
        dwr_ref[rows, STATE:] += mm_nt(
            jnp.concatenate([d_hi, d_lo, d_hi], 1), jnp.concatenate([s_hi, s_hi, s_lo], 1)
        )
        r_t = rt_ref[:, rows]
        grad = jnp.exp(end) * grad + mm(jnp.concatenate([r_t, r_t], 1), jnp.concatenate([d_hi, d_lo], 0))


def finish_kernel(*refs):
    *vp_refs, delta_ref, rate_ref, bias_ref, gd_ref, prm_ref = refs
    heads = delta_ref.shape[1]
    rate = jnp.exp(rate_ref[...])
    upper = jnp.where(iota((CHUNK, CHUNK), 1) >= iota((CHUNK, CHUNK), 0), 1.0, 0.0).astype(BF16)
    rate_sum = jnp.zeros((1, heads), F32)
    bias_sum = jnp.zeros((1, heads), F32)
    for c in range(delta_ref.shape[0] // CHUNK):
        rows = chunk_rows(c)
        vp = sum(ref[rows] for ref in vp_refs)
        hi, mid, lo = split3(vp)
        later = (mm(upper, hi) + mm(upper, mid) + mm(upper, lo))[:, :heads]
        pulled = vp[:, 2 * heads : 3 * heads]
        z = delta_ref[rows] + bias_ref[...]
        step = softplus(z)
        gate = 1.0 / (1.0 + jnp.exp(-z))
        ratio = jnp.where(step < 1e-30, 1.0, gate / jnp.maximum(step, 1e-30))
        grad = pulled * ratio - rate * later * gate
        gd_ref[rows] = grad
        rate_sum = rate_sum - rate * jnp.sum(later * step, axis=0, keepdims=True)
        bias_sum = bias_sum + jnp.sum(grad, axis=0, keepdims=True)
    prm_ref[0:1] = rate_sum
    prm_ref[1:2] = bias_sum


def params(limit_mib=40):
    return pltpu.CompilerParams(dimension_semantics=("arbitrary",), vmem_limit_bytes=limit_mib << 20)


def whole(*shape):
    return pl.BlockSpec(shape, lambda *ids: (0,) * len(shape))


def shards(
    mixer_input, write_vectors, read_vectors, delta_raw, log_rates, delta_bias, skip_gain, output_grad
):
    length, width = mixer_input.shape[1:]
    heads = delta_raw.shape[2]
    groups = write_vectors.shape[2] // STATE
    pairs = width // LANES
    per_group = pairs // groups
    group_width = width // groups
    depth = 6 * heads
    sds = jax.ShapeDtypeStruct
    x, dy = mixer_input[0], output_grad[0]
    w, r, delta = write_vectors[0], read_vectors[0], delta_raw[0]

    col = pl.BlockSpec((length, LANES), lambda j: (0, j))
    grp = pl.BlockSpec((length, STATE), lambda j: (0, j // per_group))
    grp_t = pl.BlockSpec((STATE, length), lambda j: (j // per_group, 0))
    pay_rows = 2 * STATE + TAIL
    pay, cs, ct, wt, rt = pl.pallas_call(
        functools.partial(prep_kernel, per_group=per_group),
        grid=(pairs,),
        in_specs=[col, col, grp, grp, whole(length, heads), whole(1, heads), whole(1, heads)],
        out_specs=[
            pl.BlockSpec((1, pay_rows, LANES), lambda j: (j, 0, 0)),
            whole(length, depth),
            whole(length // CHUNK, 2 * heads, CHUNK),
            grp_t,
            grp_t,
        ],
        out_shape=[
            sds((pairs, pay_rows, LANES), BF16),
            sds((length, depth), BF16),
            sds((length // CHUNK, 2 * heads, CHUNK), F32),
            sds((groups * STATE, length), BF16),
            sds((groups * STATE, length), BF16),
        ],
        compiler_params=params(),
        name="prep",
    )(x, dy, w, r, delta, log_rates, delta_bias)

    arrived = lax.all_to_all(pay, "ctx", split_axis=0, concat_axis=0, tiled=True)
    scanned = pl.pallas_call(
        scan_kernel,
        in_specs=[whole(pairs, pay_rows, LANES)],
        out_specs=whole(pairs, 2 * STATE, LANES),
        out_shape=sds((pairs, 2 * STATE, LANES), BF16),
        compiler_params=pltpu.CompilerParams(vmem_limit_bytes=40 << 20),
        grid=(1,),
        name="scan",
    )(arrived)
    edges = lax.all_to_all(scanned, "ctx", split_axis=0, concat_axis=0, tiled=True)

    skip_row = jnp.repeat(skip_gain, HEADDIM, axis=1)
    ups, vps, rows_out, skips = [], [], [], []
    for g in range(groups):
        first = g * per_group
        col_g = pl.BlockSpec((length, LANES), lambda p, first=first: (0, first + p))
        grp_g = pl.BlockSpec((length, STATE), lambda p, g=g: (0, g))
        out_col = pl.BlockSpec((length, LANES), lambda p: (0, p))
        dxi, vp, dwr, gsk = pl.pallas_call(
            functools.partial(intra_kernel, first_pair=first, heads=heads),
            grid=(per_group,),
            in_specs=[
                col_g, col_g, grp_g, grp_g, whole(length, depth), whole(length // CHUNK, 2 * heads, CHUNK),
                pl.BlockSpec((1, LANES), lambda p, first=first: (0, first + p)),
            ],
            out_specs=[out_col, whole(length, LANES), whole(length, 2 * STATE), whole(per_group, LANES)],
            out_shape=[
                sds((length, group_width), F32),
                sds((length, LANES), F32),
                sds((length, 2 * STATE), F32),
                sds((per_group, LANES), F32),
            ],
            scratch_shapes=[pltpu.VMEM((length // CHUNK, CHUNK, CHUNK), F32)] * 3,
            compiler_params=params(),
            name="intra",
        )(x, dy, w, r, cs, ct, skip_row)
        skips.append(gsk.reshape(per_group, 2, HEADDIM).sum(-1).reshape(1, -1))
        grp_tg = pl.BlockSpec((STATE, length), lambda p, g=g: (g, 0))
        up, vp, dwr = pl.pallas_call(
            functools.partial(inter_kernel, first_pair=first, heads=heads),
            grid=(per_group,),
            in_specs=[
                col_g, col_g, grp_g, grp_g, grp_tg, grp_tg, whole(length, depth),
                pl.BlockSpec((1, 2 * STATE, LANES), lambda p, first=first: (first + p, 0, 0)),
                out_col, whole(length, LANES), whole(length, 2 * STATE),
            ],
            out_specs=[out_col, whole(length, LANES), whole(length, 2 * STATE)],
            out_shape=[
                sds((length, group_width), BF16),
                sds((length, LANES), F32),
                sds((length, 2 * STATE), F32),
            ],
            scratch_shapes=[pltpu.VMEM((length // CHUNK + 1, STATE, LANES), F32)],
            compiler_params=params(),
            name="inter",
        )(x, dy, w, r, wt, rt, cs, edges, dxi, vp, dwr)
        ups.append(up)
        vps.append(vp)
        rows_out.append(dwr)

    grad_delta, sums = pl.pallas_call(
        finish_kernel,
        grid=(1,),
        in_specs=[whole(length, LANES)] * groups + [whole(length, heads), whole(1, heads), whole(1, heads)],
        out_specs=[whole(length, heads), whole(2, heads)],
        out_shape=[sds((length, heads), F32), sds((2, heads), F32)],
        compiler_params=params(),
        name="finish",
    )(*vps, delta, log_rates, delta_bias)

    devices = range(lax.axis_size("section"))
    route = [(i + 1, i) for i in devices if i + 1 in devices]
    upstream = jnp.concatenate([lax.ppermute(up, "section", route) for up in ups], axis=1)
    paired = jnp.concatenate(rows_out, axis=1)
    vector_rows = lax.all_to_all(paired, "tp", split_axis=0, concat_axis=1, tiled=True)
    mine = jnp.concatenate([sums, jnp.concatenate(skips, axis=1)], axis=0)
    places = lax.axis_size("ctx")
    spread = jnp.broadcast_to(mine[None], (places, *mine.shape))
    everyone = lax.all_to_all(spread, "ctx", split_axis=0, concat_axis=0, tiled=True)
    param_sums = jnp.sum(everyone, axis=0)
    return upstream[None], grad_delta[None], vector_rows[None], param_sums[None]


def solution(mesh):
    in_specs = (
        P("section", "ctx", "tp"),
        P("section", "ctx", "tp"),
        P("section", "ctx", "tp"),
        P("section", "ctx", "tp"),
        P("section", "tp"),
        P("section", "tp"),
        P("section", "tp"),
        P("section", "ctx", "tp"),
    )
    out_specs = (
        P("section", "ctx", "tp"),
        P("section", "ctx", "tp"),
        P("section", ("ctx", "tp"), None),
        P("section", None, "tp"),
    )
    return jax.shard_map(shards, mesh=mesh, in_specs=in_specs, out_specs=out_specs, check_vma=False)
```

time: 1030 us -> 196 us (0.19); the launches traced: 1010 us -> 192 us
  waiting for transfers between devices: 381 us -> 15.5 us
  local copies, waits for them, and re-layouts: 228 us -> 37.7 us
  matrix products: 134 us -> 0 us
  other arithmetic: 119 us -> 5.32 us
  Pallas kernels: 0 us -> 71.5 us
  loops' own time: 31.1 us -> 0 us
  blocking collectives: 64 us -> 38.4 us
  starting transfers between devices: 36.7 us -> 22.7 us
  between operations: 14.9 us -> 0.91 us
    ppermute x16 -> x2, waiting for transfers between devices: 381 us -> 0.01 us  [shards(): lax.ppermute(up, 'section', route)]
    dot_general x28 -> x0, matrix products: 134 us -> none  [the longest x4 47.2 us: advance(): within = jnp.einsum('ijgk,jgkp->igkp', weights, values, precision=HIGHEST)]
    dynamic_update_slice x14 -> x0, local copies, waits for them, and re-layouts: 124 us -> none  [block_pass(): lax.scan(jax.checkpoint(advance), start_state, blocks_in)]
    pallas_call x0 -> x7, Pallas kernels: none -> 71.5 us  [the longest x2 35.7 us: shards(): pl.pallas_call(functools.partial(inter_kernel, first_pair=first, heads=he...]
    all_to_all x0 -> x1, blocking collectives: none -> 38.4 us  [shards(): lax.all_to_all(pay, 'ctx', split_axis=0, concat_axis=0, tiled=True)]
    add x15 -> x0, other arithmetic: 35.4 us -> none  [relay_turn(): sending = entry_grad + own_decay * running]
    psum x1 -> x0, blocking collectives: 33.5 us -> none  [shards(): lax.psum(jnp.stack([grad_rate, grad_bias, grad_skip])[None], 'ctx')]
    another operation x4 -> x0, loops' own time: 31.1 us -> none  [the longest x2 30.4 us: block_pass(): lax.scan(jax.checkpoint(advance), start_state, blocks_in)]
  transfers between devices with their start and end apart: 18 -> 5, of which waited for: 15 -> 2; matrix products, arithmetic and copies ran while one was open for 10% -> 5% of each run, Pallas kernels for 0% -> 22%
where the time goes in v1:
time: 196 us; the launch traced here: 192 us
  Pallas kernels  71.5 us (36%)
  blocking collectives  38.4 us (20%)
  local copies, waits for them, and re-layouts  37.7 us (19%)
  starting transfers between devices  22.7 us (12%)
  waiting for transfers between devices  15.5 us (8%)
  other arithmetic  5.32 us (3%)
    all_to_all x1, blocking collectives, shards(): lax.all_to_all(pay, 'ctx', split_axis=0, concat_axis=0, tiled=True)  38.4 us
    pallas_call x2, Pallas kernels, shards(): pl.pallas_call(functools.partial(inter_kernel, first_pair=first, heads=he...  35.7 us
    unnamed x93, local copies, waits for them, and re-layouts  33 us
    pallas_call x2, Pallas kernels, shards(): pl.pallas_call(functools.partial(intra_kernel, first_pair=first, heads=he...  23.2 us
    pallas_call x1, Pallas kernels, shards(): pl.pallas_call(functools.partial(prep_kernel, per_group=per_group), grid=...  11.7 us
    all_to_all x1, waiting for transfers between devices, shards(): lax.all_to_all(paired, 'tp', split_axis=0, concat_axis=1, tiled=True)  10.6 us
    all_to_all x1, starting transfers between devices, shards(): lax.all_to_all(spread, 'ctx', split_axis=0, concat_axis=0, tiled=True)  8.8 us
    all_to_all x1, waiting for transfers between devices, shards(): lax.all_to_all(spread, 'ctx', split_axis=0, concat_axis=0, tiled=True)  4.97 us
  transfers between devices with their start and end apart: 5, of which 2 were waited for; matrix products, arithmetic and copies ran while one was open for 5% of the time, Pallas kernels for 22%

profile of v1, /device:TPU:50, one launch (start us, length us, event | category | flops | bytes accessed | tf_op | source)
XLA Modules:
  0.0 192.1 jit_solution(17489471865807692495)
XLA Ops:
  1.6 1.7 copy-done
  3.3 1.6 copy-done.2
  8.1 11.7 %prep.1 = (bf16[16,272,128]{2,1,0:T(8,128)(2,1)S(1)}, bf16[512,192]{1,0:T(8,128)(2,1)S(1)}, f32[4,64,128]{2,1,0:T(8,128)S(1)}, bf16[256,512]{1,0:T(8,128)(2,1)S(1)}, bf16[256,512]{1,0:T(8,128)(2,1)S(1)}) custom-call(bf16[512,2048]{1,0:T(8,128)(2,1)S(1)} %bitcast.12, bf16[512,2048]{1,0:T(8,128)(2,1)S(1)} %bitcast.17, bf16[512,256]{1,0:T(8,128)(2,1)S(1)} %bitcast.22, ...), custom_call_target="tpu_custom_call" | custom-call | tf_op jit(solution)/shard_map/prep/pallas_call | solution.py:309
  20.6 38.4 %all_to_all.31.in_ref = bf16[16,272,128]{2,1,0:T(8,128)(2,1)S(1)} all-to-all(bf16[16,272,128]{2,1,0:T(8,128)(2,1)S(1)} %get-tuple-element.28), channel_id=1, replica_groups=mesh['section'=4,'ctx'=16,'tp'=4] {'ctx'}, dimensions={0} | all-to-all | bytes 2228224 | tf_op jit(solution)/shard_map/all_to_all | solution.py:331
  60.2 4.6 %all-to-all-start.1 = ((bf16[16,256,128]{2,1,0:T(8,128)(2,1)}), bf16[16,256,128]{2,1,0:T(8,128)(2,1)S(1)}, u32[]{:S(2)}, u32[]{:S(2)}) async-start(bf16[16,256,128]{2,1,0:T(8,128)(2,1)} %copy-done.15), calls=%async_computation.1 | async-start | bytes 2097152 | tf_op jit(solution)/shard_map/all_to_all | solution.py:341
  66.3 1.6 copy-done.3
  69.7 11.6 %intra.3 = (f32[512,1024]{1,0:T(8,128)S(1)}, f32[512,128]{1,0:T(8,128)S(1)}, f32[512,256]{1,0:T(8,128)S(1)}, f32[8,128]{1,0:T(8,128)S(1)}) custom-call(bf16[512,2048]{1,0:T(8,128)(2,1)S(1)} %bitcast.13, bf16[512,2048]{1,0:T(8,128)(2,1)S(1)} %bitcast.18, bf16[512,256]{1,0:T(8,128)(2,1)S(1)} %bitcast.23, bf16[512,256]{1,0:T(8,128)(2,1)S(1)} %bitcast.28, ...), custom_call_target="tpu_custom_call" | custom-call | tf_op jit(solution)/shard_map/intra/pallas_call | solution.py:350
  81.4 1.3 copy-done.20
  84.2 11.6 %intra.2 = (f32[512,1024]{1,0:T(8,128)S(1)}, f32[512,128]{1,0:T(8,128)S(1)}, f32[512,256]{1,0:T(8,128)S(1)}, f32[8,128]{1,0:T(8,128)S(1)}) custom-call(bf16[512,2048]{1,0:T(8,128)(2,1)S(1)} %bitcast.14, bf16[512,2048]{1,0:T(8,128)(2,1)S(1)} %bitcast.19, bf16[512,256]{1,0:T(8,128)(2,1)S(1)} %bitcast.24, bf16[512,256]{1,0:T(8,128)(2,1)S(1)} %bitcast.29, ...), custom_call_target="tpu_custom_call" | custom-call | tf_op jit(solution)/shard_map/intra/pallas_call | solution.py:350
  95.8 1.3 copy-done.18
  98.7 1.6 copy-done.4
  102.2 1.6 copy-done.21
  105.7 1.0 copy-done.29
  107.7 17.8 %inter.3 = (bf16[512,1024]{1,0:T(8,128)(2,1)}, f32[512,128]{1,0:T(8,128)S(1)}, f32[512,256]{1,0:T(8,128)S(1)}) custom-call(bf16[512,2048]{1,0:T(8,128)(2,1)S(1)} %bitcast.15, bf16[512,2048]{1,0:T(8,128)(2,1)S(1)} %bitcast.20, bf16[512,256]{1,0:T(8,128)(2,1)S(1)} %bitcast.25, bf16[512,256]{1,0:T(8,128)(2,1)S(1)} %bitcast.30, bf16[256,512]{1,0:T(8,128)(2,1)S(1)} %copy-done.23, ...), custom_call_target="tpu_custom_call" | custom-call | tf_op jit(solution)/shard_map/inter/pallas_call | solution.py:370
  125.5 1.9 collective-permute-start.1
  127.5 17.9 %inter.2 = (bf16[512,1024]{1,0:T(8,128)(2,1)}, f32[512,128]{1,0:T(8,128)S(1)}, f32[512,256]{1,0:T(8,128)S(1)}) custom-call(bf16[512,2048]{1,0:T(8,128)(2,1)S(1)} %bitcast.16, bf16[512,2048]{1,0:T(8,128)(2,1)S(1)} %bitcast.21, bf16[512,256]{1,0:T(8,128)(2,1)S(1)} %bitcast.26, bf16[512,256]{1,0:T(8,128)(2,1)S(1)} %bitcast.31, bf16[256,512]{1,0:T(8,128)(2,1)S(1)} %copy-done.23, ...), custom_call_target="tpu_custom_call" | custom-call | tf_op jit(solution)/shard_map/inter/pallas_call | solution.py:370
  146.9 2.6 %collective-permute-start = (bf16[512,1024]{1,0:T(8,128)(2,1)}, bf16[512,1024]{1,0:T(8,128)(2,1)S(1)}, u32[]{:S(2)}, u32[]{:S(2)}) collective-permute-start(bf16[512,1024]{1,0:T(8,128)(2,1)} %get-tuple-element.33), channel_id=1, source_target_pairs={{64,0},{128,64},{192,128},{65,1},{129,65},{193,129},{66,2},{130,66... | collective-permute-start | bytes 3145736 | tf_op jit(solution)/shard_map/ppermute | solution.py:404
  154.2 8.8 %all-to-all-start.3 = ((f32[16,3,32]{2,1,0:T(4,128)}), f32[16,3,32]{2,1,0:T(4,128)S(1)}, u32[]{:S(2)}, u32[]{:S(2)}) async-start(f32[16,3,32]{2,1,0:T(4,128)} %broadcast_in_dim.28), calls=%async_computation.3 | async-start | bytes 65536 | tf_op jit(solution)/shard_map/all_to_all | solution.py:410
  163.0 2.3 %pad_maximum_fusion = f32[512,512]{1,0:T(8,128)} fusion(f32[512,256]{1,0:T(8,128)} %copy-done.30, f32[512,256]{1,0:T(8,128)} %copy-done.31), kind=kLoop, calls=%fused_computation.1 | loop fusion | flops 262144 | bytes 2097152 | tf_op jit(solution)/shard_map/concatenate | solution.py:405
  165.3 5.0 %all-to-all-done.3 = f32[16,3,32]{2,1,0:T(4,128)S(1)} async-done(((f32[16,3,32]{2,1,0:T(4,128)}), f32[16,3,32]{2,1,0:T(4,128)S(1)}, u32[]{:S(2)}, u32[]{:S(2)}) %all-to-all-start.3) | async-done | bytes 6176 | tf_op jit(solution)/shard_map/all_to_all | solution.py:410
  170.3 4.8 %all-to-all-start.2 = ((f32[4,128,512]{2,1,0:T(8,128)}), f32[4,128,512]{2,1,0:T(8,128)S(1)}, u32[]{:S(2)}, u32[]{:S(2)}) async-start(f32[4,128,512]{2,1,0:T(8,128)} %bitcast.8), calls=%async_computation.2 | async-start | bytes 2097152 | tf_op jit(solution)/shard_map/all_to_all | solution.py:406
  176.4 10.6 %all-to-all-done.2 = f32[4,128,512]{2,1,0:T(8,128)S(1)} async-done(((f32[4,128,512]{2,1,0:T(8,128)}), f32[4,128,512]{2,1,0:T(8,128)S(1)}, u32[]{:S(2)}, u32[]{:S(2)}) %all-to-all-start.2) | async-done | bytes 1048608 | tf_op jit(solution)/shard_map/all_to_all | solution.py:406
  187.7 1.7 broadcast_in_dim.27
  189.4 2.8 %maximum_bitcast_fusion = bf16[1,512,2048]{2,1,0:T(8,128)(2,1)} fusion(bf16[512,1024]{1,0:T(8,128)(2,1)} %collective-permute-done.1, bf16[512,1024]{1,0:T(8,128)(2,1)S(1)} %collective-permute-done), kind=kLoop, calls=%fused_computation | loop fusion | flops 4194304 | bytes 4194304 | tf_op jit(solution)/shard_map/broadcast_in_dim | solution.py:412
  (102 shorter events, 25.5 us)
Async XLA Ops:
  1.6 18.3 %copy-start.16 = (f32[1,512,32]{2,1,0:T(8,128)}, f32[1,512,32]{2,1,0:T(8,128)S(1)}, u32[]{:S(2)}) copy-start(f32[1,512,32]{2,1,0:T(8,128)S(1)} %copy.24) | copy-start | bytes 196612
  1.6 1.7 copy-start
  20.6 38.4 %copy-start.22 = (bf16[256,512]{1,0:T(8,128)(2,1)}, bf16[256,512]{1,0:T(8,128)(2,1)S(1)}, u32[]{:S(2)}) copy-start(bf16[256,512]{1,0:T(8,128)(2,1)S(1)} %get-tuple-element.25.wt_ref) | copy-start | bytes 786436
  20.6 38.4 %copy-start.24 = (bf16[256,512]{1,0:T(8,128)(2,1)}, bf16[256,512]{1,0:T(8,128)(2,1)S(1)}, u32[]{:S(2)}) copy-start(bf16[256,512]{1,0:T(8,128)(2,1)S(1)} %get-tuple-element.26.rt_ref) | copy-start | bytes 786436
  58.9 5.8 %copy-start.44 = (f32[1,32]{1,0:T(1,128)S(1)}, f32[1,32]{1,0:T(1,128)}, u32[]{:S(2)}) copy-start(f32[1,32]{1,0:T(1,128)} %param.14) | copy-start | bytes 388
  58.9 7.3 %copy-start.1 = (bf16[1,512,2048]{2,1,0:T(8,128)(2,1)S(1)}, bf16[1,512,2048]{2,1,0:T(8,128)(2,1)}, u32[]{:S(2)}) copy-start(bf16[1,512,2048]{2,1,0:T(8,128)(2,1)} %param.8) | copy-start | bytes 6291460
  58.9 7.3 %copy-start.6 = (bf16[1,512,256]{2,1,0:T(8,128)(2,1)S(1)}, bf16[1,512,256]{2,1,0:T(8,128)(2,1)}, u32[]{:S(2)}) copy-start(bf16[1,512,256]{2,1,0:T(8,128)(2,1)} %param.9) | copy-start | bytes 786436
  60.2 38.5 %all-to-all-start.1 = ((bf16[16,256,128]{2,1,0:T(8,128)(2,1)}), bf16[16,256,128]{2,1,0:T(8,128)(2,1)S(1)}, u32[]{:S(2)}, u32[]{:S(2)}) async-start(bf16[16,256,128]{2,1,0:T(8,128)(2,1)} %copy-done.15), calls=%async_computation.1 | async-start | bytes 2097152 | tf_op jit(solution)/shard_map/all_to_all | solution.py:341
  66.3 1.6 copy-start.3
  98.7 1.6 copy-start.4
  102.2 1.6 copy-start.21
  107.7 19.8 %copy-start.10 = (bf16[1,512,256]{2,1,0:T(8,128)(2,1)S(1)}, bf16[1,512,256]{2,1,0:T(8,128)(2,1)}, u32[]{:S(2)}) copy-start(bf16[1,512,256]{2,1,0:T(8,128)(2,1)} %param.10) | copy-start | bytes 786436
  107.7 19.8 %copy-start.14 = (bf16[512,192]{1,0:T(8,128)(2,1)S(1)}, bf16[512,192]{1,0:T(8,128)(2,1)}, u32[]{:S(2)}) copy-start(bf16[512,192]{1,0:T(8,128)(2,1)} %copy-done.11) | copy-start | bytes 589828
  107.7 19.8 %copy-start.19 = (f32[512,1024]{1,0:T(8,128)S(1)}, f32[512,1024]{1,0:T(8,128)}, u32[]{:S(2)}) copy-start(f32[512,1024]{1,0:T(8,128)} %copy-done.18) | copy-start | bytes 6291460
  107.7 19.8 %copy-start.27 = (f32[512,256]{1,0:T(8,128)S(1)}, f32[512,256]{1,0:T(8,128)}, u32[]{:S(2)}) copy-start(f32[512,256]{1,0:T(8,128)} %copy-done.26) | copy-start | bytes 1572868
  107.7 19.8 %copy-start.33 = (f32[512,128]{1,0:T(8,128)S(1)}, f32[512,128]{1,0:T(8,128)}, u32[]{:S(2)}) copy-start(f32[512,128]{1,0:T(8,128)} %copy-done.32) | copy-start | bytes 786436
  125.5 19.9 %copy-start.30 = (f32[512,256]{1,0:T(8,128)}, f32[512,256]{1,0:T(8,128)S(1)}, u32[]{:S(2)}) copy-start(f32[512,256]{1,0:T(8,128)S(1)} %get-tuple-element.42) | copy-start | bytes 1572868
  125.5 19.9 %copy-start.36 = (f32[512,128]{1,0:T(8,128)}, f32[512,128]{1,0:T(8,128)S(1)}, u32[]{:S(2)}) copy-start(f32[512,128]{1,0:T(8,128)S(1)} %get-tuple-element.39.refs_1_) | copy-start | bytes 786436
  125.5 63.9 %collective-permute-start.1 = (bf16[512,1024]{1,0:T(8,128)(2,1)}, bf16[512,1024]{1,0:T(8,128)(2,1)}, u32[]{:S(2)}, u32[]{:S(2)}) collective-permute-start(bf16[512,1024]{1,0:T(8,128)(2,1)} %get-tuple-element.37), channel_id=1, source_target_pairs={{64,0},{128,64},{192,128},{65,1},{129,65},{193,129},{66,2},{130,66... | collective-permute-start | bytes 3145736 | tf_op jit(solution)/shard_map/ppermute | solution.py:404
  127.5 22.6 %copy-start.41 = (f32[1,32]{1,0:T(1,128)S(1)}, f32[1,32]{1,0:T(1,128)}, u32[]{:S(2)}) copy-start(f32[1,32]{1,0:T(1,128)} %refs_3_.1) | copy-start | bytes 388
  127.5 22.5 %copy-start.43 = (f32[1,32]{1,0:T(1,128)S(1)}, f32[1,32]{1,0:T(1,128)}, u32[]{:S(2)}) copy-start(f32[1,32]{1,0:T(1,128)} %refs_4_.1) | copy-start | bytes 388
  146.9 42.5 %collective-permute-start = (bf16[512,1024]{1,0:T(8,128)(2,1)}, bf16[512,1024]{1,0:T(8,128)(2,1)S(1)}, u32[]{:S(2)}, u32[]{:S(2)}) collective-permute-start(bf16[512,1024]{1,0:T(8,128)(2,1)} %get-tuple-element.33), channel_id=1, source_target_pairs={{64,0},{128,64},{192,128},{65,1},{129,65},{193,129},{66,2},{130,66... | collective-permute-start | bytes 3145736 | tf_op jit(solution)/shard_map/ppermute | solution.py:404
  154.2 16.0 %all-to-all-start.3 = ((f32[16,3,32]{2,1,0:T(4,128)}), f32[16,3,32]{2,1,0:T(4,128)S(1)}, u32[]{:S(2)}, u32[]{:S(2)}) async-start(f32[16,3,32]{2,1,0:T(4,128)} %broadcast_in_dim.28), calls=%async_computation.3 | async-start | bytes 65536 | tf_op jit(solution)/shard_map/all_to_all | solution.py:410
  170.3 16.7 %all-to-all-start.2 = ((f32[4,128,512]{2,1,0:T(8,128)}), f32[4,128,512]{2,1,0:T(8,128)S(1)}, u32[]{:S(2)}, u32[]{:S(2)}) async-start(f32[4,128,512]{2,1,0:T(8,128)} %bitcast.8), calls=%async_computation.2 | async-start | bytes 2097152 | tf_op jit(solution)/shard_map/all_to_all | solution.py:406
  (26 other events, 24.2 us)

commit v2 on v1

v2 whole, which is shorter than its diff:
```python
import functools

import jax
import jax.numpy as jnp
from jax import lax
from jax.experimental import pallas as pl
from jax.experimental.pallas import tpu as pltpu
from jax.sharding import PartitionSpec as P


HEADDIM = 64
STATE = 128
CHUNK = 128
LANES = 128
F32 = jnp.float32
BF16 = jnp.bfloat16
TAIL = 8


def iota(shape, dim):
    return lax.broadcasted_iota(jnp.int32, shape, dim)


def mm(a, b):
    return lax.dot_general(a, b, (((1,), (0,)), ((), ())), preferred_element_type=F32)


def mm_nt(a, b):
    return lax.dot_general(a, b, (((1,), (1,)), ((), ())), preferred_element_type=F32)


def split2(v):
    hi = v.astype(BF16)
    return hi, (v - hi.astype(F32)).astype(BF16)


def split3(v):
    hi = v.astype(BF16)
    rest = v - hi.astype(F32)
    mid = rest.astype(BF16)
    return hi, mid, (rest - mid.astype(F32)).astype(BF16)


def softplus(z):
    u = jnp.exp(-jnp.abs(z))
    small = u * (1.0 - u * (0.5 - u * (1.0 / 3.0 - u * (0.25 - u * 0.2))))
    return jnp.maximum(z, 0.0) + jnp.where(u < 0.03, small, jnp.log(1.0 + u))


def chunk_rows(c):
    return slice(c * CHUNK, (c + 1) * CHUNK)


def fill_expand_base(base_ref, heads):
    row, col = iota(base_ref.shape, 0), iota(base_ref.shape, 1)
    width = base_ref.shape[1] // 2
    kind = (row & (2 * heads - 1)) >= heads
    place = (col & (width - 1)) // HEADDIM
    base_ref[...] = jnp.where(kind == (col >= width), (row & (heads - 1)) - place, -64)


def expand(split, base_ref, first_head):
    hit = jnp.where(base_ref[...] == first_head, 1.0, 0.0).astype(BF16)
    out = mm(split, hit)
    width = out.shape[1] // 2
    return out[:, :width], out[:, width:]


def fill_sum_base(base_ref):
    row, col = iota(base_ref.shape, 0), iota(base_ref.shape, 1)
    base_ref[...] = col - (row & (LANES - 1)) // HEADDIM


def sum_pick(base_ref, column):
    return jnp.where(base_ref[...] == column, 1.0, 0.0).astype(BF16)


def head_sum(product, pick):
    return mm(jnp.concatenate(split2(product), axis=1), pick)


def row_ends(cl, chunks):
    return [cl[(c + 1) * CHUNK - 1 : (c + 1) * CHUNK] for c in range(chunks)]


def running(ends):
    before = [jnp.zeros_like(ends[0])]
    for end in ends:
        before.append(before[-1] + end)
    return before


def as_columns(row_ref, width):
    return jnp.concatenate([jnp.broadcast_to(row_ref[...], (LANES, row_ref.shape[1])).T] * (width // LANES), 1)


def prep_kernel(
    x_ref, dy_ref, w_ref, r_ref, delta_ref, rate_ref, bias_ref,
    pay_ref, low_ref, cs_ref, ct_ref, wt_ref, rt_ref, base_ref, *, steps_per_group
):
    quad = pl.program_id(0)
    length = x_ref.shape[0]
    heads = delta_ref.shape[0]
    chunks = length // CHUNK

    @pl.when(quad == 0)
    def _():
        fill_expand_base(base_ref, heads)
        step = softplus(delta_ref[...] + as_columns(bias_ref, length))
        logs = jnp.maximum(jnp.log(step), -200.0)
        decay = -step * jnp.exp(as_columns(rate_ref, length))
        upto = jnp.where(iota((CHUNK, CHUNK), 0) <= iota((CHUNK, CHUNK), 1), 1.0, 0.0).astype(BF16)
        for c in range(chunks):
            hi, mid, lo = split3(decay[:, chunk_rows(c)])
            cum = mm(hi, upto) + mm(mid, upto) + mm(lo, upto)
            both = jnp.concatenate([cum, cum - logs[:, chunk_rows(c)]], axis=0)
            ct_ref[c] = both
            cs_ref[chunk_rows(c), :] = jnp.concatenate(split3(both.T), axis=1)

    @pl.when(quad % steps_per_group == 0)
    def _():
        wt_ref[...] = w_ref[...].astype(F32).T.astype(BF16)
        rt_ref[...] = r_ref[...].astype(F32).T.astype(BF16)

    cl, ll = expand(cs_ref[...], base_ref, quad * (2 * LANES // HEADDIM))
    before = running(row_ends(cl, chunks))
    total = before[chunks]
    state = jnp.zeros((STATE, 2 * LANES), F32)
    grad = jnp.zeros((STATE, 2 * LANES), F32)
    for c in range(chunks):
        rows = chunk_rows(c)
        drawn = x_ref[rows].astype(F32) * jnp.exp((total - before[c]) - ll[rows])
        w_t, r_t = wt_ref[:, rows], rt_ref[:, rows]
        state += mm(jnp.concatenate([w_t, w_t], 1), jnp.concatenate(split2(drawn), 0))
        pushed = dy_ref[rows].astype(F32) * jnp.exp(before[c] + cl[rows])
        grad += mm(jnp.concatenate([r_t, r_t], 1), jnp.concatenate(split2(pushed), 0))
    carry = jnp.exp(total)
    carry_hi = carry.astype(BF16).astype(F32)
    picked = jnp.where(iota((TAIL, 2 * LANES), 0) == 0, carry_hi, carry - carry_hi).astype(BF16)
    state_hi, state_lo = split2(state)
    grad = grad.astype(BF16)
    for k in range(2):
        lanes = slice(k * LANES, (k + 1) * LANES)
        pay_ref[k, :STATE] = state_hi[:, lanes]
        pay_ref[k, STATE : 2 * STATE] = grad[:, lanes]
        pay_ref[k, 2 * STATE :] = picked[:, lanes]
        low_ref[k] = state_lo[:, lanes]


def scan_kernel(in_ref, out_ref):
    places = in_ref.shape[0]

    def carry(c):
        tail = in_ref[c, 2 * STATE :].astype(F32)
        return tail[0:1] + tail[1:2]

    state = jnp.zeros((STATE, LANES), F32)
    for c in range(places):
        out_ref[c, :STATE] = state.astype(BF16)
        state = carry(c) * state + in_ref[c, :STATE].astype(F32)
    grad = jnp.zeros((STATE, LANES), F32)
    for c in reversed(range(places)):
        out_ref[c, STATE:] = grad.astype(BF16)
        grad = carry(c) * grad + in_ref[c, STATE : 2 * STATE].astype(F32)


def local_kernel(
    x_ref, dy_ref, w_ref, r_ref, wt_ref, rt_ref, cs_ref, ct_ref, skip_ref,
    dxi_ref, vp_ref, dwr_ref, gsk_ref, pushed_ref, drawn_ref, tail_ref,
    sc_ref, sct_ref, dsc_ref, states_ref, base_ref, sum_base_ref, *, first_pair, heads
):
    place = pl.program_id(0)
    pair = first_pair + place
    length = x_ref.shape[0]
    chunks = length // CHUNK

    @pl.when(place == 0)
    def _():
        for c in range(chunks):
            rows = chunk_rows(c)
            sc_ref[c] = mm_nt(r_ref[rows], w_ref[rows])
            sct_ref[c] = mm_nt(w_ref[rows], r_ref[rows])
        dsc_ref[...] = jnp.zeros_like(dsc_ref)
        vp_ref[...] = jnp.zeros_like(vp_ref)
        dwr_ref[...] = jnp.zeros_like(dwr_ref)
        gsk_ref[...] = jnp.zeros_like(gsk_ref)
        fill_expand_base(base_ref, heads)
        fill_sum_base(sum_base_ref)

    cl, ll = expand(cs_ref[...], base_ref, 2 * pair)
    pick_push = sum_pick(sum_base_ref, 2 * pair)
    pick_drawn = sum_pick(sum_base_ref, 2 * heads + 2 * pair)
    row, col = iota((CHUNK, CHUNK), 0), iota((CHUNK, CHUNK), 1)
    left = iota((CHUNK, LANES), 1) < HEADDIM
    left_b = jnp.where(left, 1.0, 0.0).astype(BF16)
    right_b = jnp.where(left, 0.0, 1.0).astype(BF16)
    skip_sum = jnp.zeros((1, LANES), F32)
    ends = row_ends(cl, chunks)
    before = running(ends)

    state = None
    for c in range(chunks - 1):
        rows = chunk_rows(c)
        hi, lo = split2(x_ref[rows].astype(F32) * jnp.exp(ends[c] - ll[rows]))
        w_t = wt_ref[:, rows]
        written = mm(jnp.concatenate([w_t, w_t], 1), jnp.concatenate([hi, lo], 0))
        state = written if state is None else jnp.exp(ends[c]) * state + written
        states_ref[c + 1] = state

    grad = None
    for c in reversed(range(chunks)):
        rows = chunk_rows(c)
        x, dy = x_ref[rows], dy_ref[rows]
        xf, dyf = x.astype(F32), dy.astype(F32)
        x_two = jnp.concatenate([x * left_b, x * right_b], axis=0)
        dy_two = jnp.concatenate([dy * left_b, dy * right_b], axis=0)
        gram = mm_nt(dy, x_two)
        mixes, mixes_t = [], []
        total = dsc_ref[c]
        for k in range(2):
            lane = slice(k * HEADDIM, k * HEADDIM + 1)
            log_row = ct_ref[c, pl.ds(heads + 2 * pair + k, 1), :]
            decay = jnp.exp(jnp.where(row >= col, cl[rows, lane] - log_row, -1e30))
            mixes.append((sc_ref[c] * decay).astype(BF16))
            total = total + gram[:, k * CHUNK : (k + 1) * CHUNK] * decay
            cum_row = ct_ref[c, pl.ds(2 * pair + k, 1), :]
            decay_t = jnp.exp(jnp.where(col >= row, cum_row - ll[rows, lane], -1e30))
            mixes_t.append((sct_ref[c] * decay_t).astype(BF16))
        dsc_ref[c] = total
        y = mm(jnp.concatenate(mixes, axis=1), x_two)
        dx = mm(jnp.concatenate(mixes_t, axis=1), dy_two)
        seen = jnp.exp(cl[rows])
        pulled_y = dyf * seen
        if c > 0:
            r = r_ref[rows]
            s_hi, s_lo = split2(states_ref[c])
            y = y + seen * mm(jnp.concatenate([r, r], 1), jnp.concatenate([s_hi, s_lo], 0))
            d_hi, d_lo = split2(pulled_y)
            dwr_ref[rows, STATE:] += mm_nt(d_hi, s_hi)
        if grad is not None:
            w = w_ref[rows]
            tail = jnp.exp(ends[c] - ll[rows])
            g_hi, g_lo = split2(grad)
            dx = dx + tail * mm(jnp.concatenate([w, w], 1), jnp.concatenate([g_hi, g_lo], 0))
            dwr_ref[rows, :STATE] += mm_nt((xf * tail).astype(BF16), g_hi)
        if c > 0:
            r_t = rt_ref[:, rows]
            pulled = mm(jnp.concatenate([r_t, r_t], 1), jnp.concatenate([d_hi, d_lo], 0))
            grad = pulled if grad is None else jnp.exp(ends[c]) * grad + pulled
        drawn = xf * dx
        vp_ref[rows] += head_sum(dyf * y - drawn, pick_push) + head_sum(drawn, pick_drawn)
        dxi_ref[0, rows] = dx + skip_ref[...] * dyf
        skip_sum = skip_sum + jnp.sum(xf * dyf, axis=0, keepdims=True)
        pushed_ref[0, rows] = jnp.concatenate(split2(dyf * jnp.exp(before[c] + cl[rows])), 1)
        tail = jnp.exp((before[chunks] - before[c]) - ll[rows])
        drawn_ref[0, rows] = jnp.concatenate(split2(xf * tail), 1)
        tail_ref[0, rows] = tail
    gsk_ref[...] += head_sum(jnp.broadcast_to(skip_sum, (gsk_ref.shape[0], LANES)), pick_push)

    @pl.when(place == pl.num_programs(0) - 1)
    def _():
        for c in range(chunks):
            rows = chunk_rows(c)
            w, r = w_ref[rows], r_ref[rows]
            total = dsc_ref[c]
            hi, lo = split2(total)
            dwr_ref[rows, STATE:] += mm(jnp.concatenate([hi, lo], 1), jnp.concatenate([w, w], 0))
            hi, lo = split2(total.T)
            dwr_ref[rows, :STATE] += mm(jnp.concatenate([hi, lo], 1), jnp.concatenate([r, r], 0))


def inter_kernel(
    pushed_ref, drawn_ref, tail_ref, w_ref, r_ref, pay_ref, low_ref, st_ref, dxi_ref, vp_in_ref,
    gsk_ref, delta_ref, rate_ref, bias_ref, *refs, first_pair, heads, copies
):
    *refs, up_ref, gd_ref, prm_ref, vp_ref, sum_base_ref = refs
    place = pl.program_id(0)
    batch, length = pushed_ref.shape[:2]

    @pl.when(place == 0)
    def _():
        vp_ref[...] = vp_in_ref[...]
        fill_sum_base(sum_base_ref)

    sums = None
    for k in range(batch):
        pair = first_pair + place * batch + k
        state, grad = st_ref[k, :STATE], st_ref[k, STATE:]
        mark = pay_ref[k, 2 * STATE :].astype(F32)
        own = pay_ref[k, :STATE].astype(F32) + low_ref[k].astype(F32)
        ending = own + (mark[0:1] + mark[1:2]) * state.astype(F32)
        edge = jnp.sum(ending * grad.astype(F32), axis=0, keepdims=True)
        pushed, drawn = pushed_ref[k], drawn_ref[k]
        y = mm(r_ref[...], state)
        dx = mm(w_ref[...], grad)
        pulled = (drawn[:, :LANES].astype(F32) + drawn[:, LANES:].astype(F32)) * dx
        push = (pushed[:, :LANES].astype(F32) + pushed[:, LANES:].astype(F32)) * y - pulled
        push = push + jnp.where(iota((length, LANES), 0) == length - 1, edge, 0.0)
        found = head_sum(push, sum_pick(sum_base_ref, 2 * pair))
        found = found + head_sum(pulled, sum_pick(sum_base_ref, 2 * heads + 2 * pair))
        sums = found if sums is None else sums + found
        up_ref[:, k * LANES : (k + 1) * LANES] = (dxi_ref[k] + tail_ref[k] * dx).astype(BF16)
    vp_ref[...] += sums

    @pl.when(place == pl.num_programs(0) - 1)
    def _():
        rate = jnp.exp(as_columns(rate_ref, CHUNK))
        bias = as_columns(bias_ref, CHUNK)
        after = jnp.where(iota((CHUNK, CHUNK), 0) >= iota((CHUNK, CHUNK), 1), 1.0, 0.0).astype(BF16)
        rate_sum = jnp.zeros((heads, CHUNK), F32)
        bias_sum = jnp.zeros((heads, CHUNK), F32)
        beyond = jnp.zeros((heads, 1), F32)
        for c in reversed(range(length // CHUNK)):
            rows = chunk_rows(c)
            vp = vp_ref[rows].T
            hi, mid, lo = split3(vp[:heads])
            later = mm(hi, after) + mm(mid, after) + mm(lo, after) + beyond
            beyond = later[:, 0:1]
            z = delta_ref[:, rows] + bias
            step = softplus(z)
            gate = 1.0 / (1.0 + jnp.exp(-z))
            ratio = jnp.where(step < 1e-30, 1.0, gate / jnp.maximum(step, 1e-30))
            grad_delta = vp[2 * heads : 3 * heads] * ratio - rate * later * gate
            rate_sum = rate_sum - rate * later * step
            bias_sum = bias_sum + grad_delta
            if first_pair:
                grad_delta = grad_delta + refs[0][:, rows]
            gd_ref[:, rows] = grad_delta
        lane = iota((heads, LANES), 1)
        rate_sum = jnp.sum(rate_sum, axis=1, keepdims=True)
        bias_sum = jnp.sum(bias_sum, axis=1, keepdims=True)
        both = jnp.where(lane == 0, rate_sum, jnp.where(lane == 1, bias_sum, 0.0))
        both = jnp.concatenate([both, jnp.zeros((LANES - heads, LANES), F32)], 0).T[:8]
        sums = jnp.where(iota((8, LANES), 0) == 2, gsk_ref[...], both)
        if first_pair:
            sums = sums + refs[1][0]
        for k in range(copies):
            prm_ref[k] = sums


def vectors_kernel(me_ref, *refs, groups, places):
    out_refs, sum_ref = refs[4 * groups : -1], refs[-1]
    place = pl.program_id(0)
    length = refs[0].shape[1]
    for g in range(groups):
        pushed_ref, drawn_ref, st_ref, dwr_ref = refs[4 * g : 4 * g + 4]
        cols = slice(g * 2 * STATE, (g + 1) * 2 * STATE)

        @pl.when(place == 0)
        def _():
            sum_ref[:, cols] = dwr_ref[...]

        batch = pushed_ref.shape[0]
        half = g * 2 * STATE + STATE
        for ref, cols, part in (
            (drawn_ref, slice(half - STATE, half), slice(STATE, 2 * STATE)),
            (pushed_ref, slice(half, half + STATE), slice(0, STATE)),
        ):
            left = jnp.concatenate([ref[k] for k in range(batch)], axis=1)
            right = jnp.concatenate([st_ref[k, part] for k in range(batch) for _ in range(2)], axis=1)
            sum_ref[:, cols] += mm_nt(left, right)

    @pl.when(place == pl.num_programs(0) - 1)
    def _():
        rows = length // places
        for hop in range(places):
            start = pl.multiple_of(lax.rem(me_ref[0] + hop, places) * rows, rows)
            out_refs[hop][...] = sum_ref[pl.ds(start, rows), :].astype(BF16)


def rows_kernel(me_ref, *refs):
    *in_refs, out_ref = refs
    places = len(in_refs)
    width = in_refs[0].shape[1]
    for hop, ref in enumerate(in_refs):
        source = lax.rem(me_ref[0] + (places - hop), places)
        out_ref[:, pl.ds(pl.multiple_of(source * width, width), width)] = ref[...].astype(F32)


def params():
    return pltpu.CompilerParams(dimension_semantics=("arbitrary",), vmem_limit_bytes=67043328)


def cost(flops, moved):
    return pl.CostEstimate(flops=flops, bytes_accessed=moved, transcendentals=0)


def whole(*shape):
    return pl.BlockSpec(shape, lambda *ids: (0,) * len(shape))


def shards(
    mixer_input, write_vectors, read_vectors, delta_raw, log_rates, delta_bias, skip_gain, output_grad
):
    length, width = mixer_input.shape[1:]
    heads = delta_raw.shape[2]
    groups = write_vectors.shape[2] // STATE
    pairs = width // LANES
    per_group = pairs // groups
    group_width = width // groups
    depth = 6 * heads
    sds = jax.ShapeDtypeStruct
    x, dy = mixer_input[0], output_grad[0]
    w, r, delta = write_vectors[0], read_vectors[0], delta_raw[0].T

    steps = pairs // 2
    steps_per_group = steps // groups
    col = pl.BlockSpec((length, 2 * LANES), lambda j: (0, j))
    grp = pl.BlockSpec((length, STATE), lambda j: (0, j // steps_per_group))
    grp_t = pl.BlockSpec((STATE, length), lambda j: (j // steps_per_group, 0))
    pay_rows = 2 * STATE + TAIL
    pay, low, cs, ct, wt, rt = pl.pallas_call(
        functools.partial(prep_kernel, steps_per_group=steps_per_group),
        grid=(steps,),
        in_specs=[col, col, grp, grp, whole(heads, length), whole(1, heads), whole(1, heads)],
        out_specs=[
            pl.BlockSpec((2, pay_rows, LANES), lambda j: (j, 0, 0)),
            pl.BlockSpec((2, STATE, LANES), lambda j: (j, 0, 0)),
            whole(length, depth),
            whole(length // CHUNK, 2 * heads, CHUNK),
            grp_t,
            grp_t,
        ],
        out_shape=[
            sds((pairs, pay_rows, LANES), BF16),
            sds((pairs, STATE, LANES), BF16),
            sds((length, depth), BF16),
            sds((length // CHUNK, 2 * heads, CHUNK), F32),
            sds((groups * STATE, length), BF16),
            sds((groups * STATE, length), BF16),
        ],
        scratch_shapes=[pltpu.VMEM((depth, 4 * LANES), jnp.int32)],
        compiler_params=params(),
        name="prep",
    )(x, dy, w, r, delta, log_rates, delta_bias)

    skip_row = jnp.repeat(skip_gain, HEADDIM, axis=1)
    own_col = pl.BlockSpec((1, length, LANES), lambda p: (p, 0, 0))
    own_two = pl.BlockSpec((1, length, 2 * LANES), lambda p: (p, 0, 0))
    batch = 2
    trips = per_group // batch

    def many(*shape):
        return pl.BlockSpec((batch, *shape), lambda p: (p, 0, 0))

    def many_of(g, *shape):
        return pl.BlockSpec((batch, *shape), lambda p: (g * trips + p, 0, 0))

    me = lax.axis_index("tp")[None]
    places, copies = lax.axis_size("tp"), lax.axis_size("ctx")

    def group_specs(g):
        first = g * per_group
        col_g = pl.BlockSpec((length, LANES), lambda p: (0, first + p))
        grp_g = pl.BlockSpec((length, STATE), lambda p: (0, g))
        grp_tg = pl.BlockSpec((STATE, length), lambda p: (g, 0))
        return first, col_g, grp_g, grp_tg

    def local(g, cs):
        first, col_g, grp_g, grp_tg = group_specs(g)
        return pl.pallas_call(
            functools.partial(local_kernel, first_pair=first, heads=heads),
            grid=(per_group,),
            in_specs=[
                col_g, col_g, grp_g, grp_g, grp_tg, grp_tg, whole(length, depth),
                whole(length // CHUNK, 2 * heads, CHUNK),
                pl.BlockSpec((1, LANES), lambda p: (0, first + p)),
            ],
            out_specs=[
                own_col, whole(length, LANES), whole(length, 2 * STATE), whole(8, LANES), own_two, own_two, own_col
            ],
            out_shape=[
                sds((per_group, length, LANES), F32),
                sds((length, LANES), F32),
                sds((length, 2 * STATE), F32),
                sds((8, LANES), F32),
                sds((per_group, length, 2 * LANES), BF16),
                sds((per_group, length, 2 * LANES), BF16),
                sds((per_group, length, LANES), F32),
            ],
            scratch_shapes=[pltpu.VMEM((length // CHUNK, CHUNK, CHUNK), F32)] * 4
            + [pltpu.VMEM((depth, 2 * LANES), jnp.int32), pltpu.VMEM((2 * LANES, LANES), jnp.int32)],
            compiler_params=params(),
            cost_estimate=cost(20 * 10**9, 64 << 20),
            name="local",
        )(x, dy, w, r, wt, rt, cs, ct, skip_row)

    def inter(g, edges, own, carried):
        first, _, grp_g, _ = group_specs(g)
        dxi, vp, _, gsk, pushed, drawn, tail = own
        mine = copies if g == groups - 1 else 1
        return pl.pallas_call(
            functools.partial(inter_kernel, first_pair=first, heads=heads, copies=mine),
            grid=(trips,),
            in_specs=[
                many(length, 2 * LANES), many(length, 2 * LANES), many(length, LANES), grp_g, grp_g,
                many_of(g, pay_rows, LANES), many_of(g, STATE, LANES), many_of(g, 2 * STATE, LANES),
                many(length, LANES), whole(length, LANES), whole(8, LANES),
                whole(heads, length), whole(1, heads), whole(1, heads), *[whole(*a.shape) for a in carried],
            ],
            out_specs=[
                pl.BlockSpec((length, batch * LANES), lambda p: (0, p)), whole(heads, length), whole(mine, 8, LANES)
            ],
            out_shape=[sds((length, group_width), BF16), sds((heads, length), F32), sds((mine, 8, LANES), F32)],
            scratch_shapes=[pltpu.VMEM((length, LANES), F32), pltpu.VMEM((2 * LANES, LANES), jnp.int32)],
            compiler_params=params(),
            cost_estimate=cost(4 * 10**9, 16 << 20),
            name="inter",
        )(pushed, drawn, tail, w, r, pay, low, edges, dxi, vp, gsk, delta, log_rates, delta_bias, *carried)

    arrived = lax.all_to_all(pay, "ctx", split_axis=0, concat_axis=0, tiled=True)
    own = [local(0, cs)]
    arrived, own[0] = lax.optimization_barrier((arrived, own[0]))
    scanned = pl.pallas_call(
        scan_kernel,
        in_specs=[whole(pairs, pay_rows, LANES)],
        out_specs=whole(pairs, 2 * STATE, LANES),
        out_shape=sds((pairs, 2 * STATE, LANES), BF16),
        compiler_params=params(),
        grid=(1,),
        name="scan",
    )(arrived)
    scanned, cs_later = lax.optimization_barrier((scanned, cs))
    edges = lax.all_to_all(scanned, "ctx", split_axis=0, concat_axis=0, tiled=True)
    own += [local(g, cs_later) for g in range(1, groups)]
    edges, own = lax.optimization_barrier((edges, own))

    devices = range(lax.axis_size("section"))
    route = [(i + 1, i) for i in devices if i + 1 in devices]
    ups, carried = [], []
    for g in range(groups):
        up, *carried = inter(g, edges, own[g], carried)
        ups.append(lax.ppermute(up, "section", route))
    grad_delta, sums = carried
    everyone = lax.all_to_all(sums, "ctx", split_axis=0, concat_axis=0, tiled=True)

    param_sums = jnp.sum(everyone, axis=0)[:3, :heads]
    upstream = jnp.concatenate(ups, axis=1)
    row_shape = (length // places, groups * 2 * STATE)
    pieces = [a for g in range(groups) for a in (own[g][4], own[g][5], edges, own[g][2])]
    row_blocks = pl.pallas_call(
        functools.partial(vectors_kernel, groups=groups, places=places),
        grid=(trips,),
        in_specs=[pl.BlockSpec(memory_space=pltpu.SMEM)]
        + [
            spec
            for g in range(groups)
            for spec in (
                many(length, 2 * LANES), many(length, 2 * LANES), many_of(g, 2 * STATE, LANES), whole(length, 2 * STATE)
            )
        ],
        out_specs=[whole(*row_shape)] * places,
        out_shape=[sds(row_shape, BF16)] * places,
        scratch_shapes=[pltpu.VMEM((length, row_shape[1]), F32)],
        compiler_params=params(),
        cost_estimate=cost(4 * 10**9, 16 << 20),
        name="vectors",
    )(me, *pieces)
    got = [
        lax.ppermute(part, "tp", [(i, (i + hop) % places) for i in range(places)]) if hop else part
        for hop, part in enumerate(row_blocks)
    ]
    upstream, param_sums, got = lax.optimization_barrier((upstream, param_sums, got))
    vector_rows = pl.pallas_call(
        rows_kernel,
        grid=(1,),
        in_specs=[pl.BlockSpec(memory_space=pltpu.SMEM)] + [whole(*row_shape)] * places,
        out_specs=whole(row_shape[0], row_shape[1] * places),
        out_shape=sds((row_shape[0], row_shape[1] * places), F32),
        compiler_params=params(),
        name="rows",
    )(me, *got)
    return upstream[None], grad_delta.T[None], vector_rows[None], param_sums[None]


def solution(mesh):
    in_specs = (
        P("section", "ctx", "tp"),
        P("section", "ctx", "tp"),
        P("section", "ctx", "tp"),
        P("section", "ctx", "tp"),
        P("section", "tp"),
        P("section", "tp"),
        P("section", "tp"),
        P("section", "ctx", "tp"),
    )
    out_specs = (
        P("section", "ctx", "tp"),
        P("section", "ctx", "tp"),
        P("section", ("ctx", "tp"), None),
        P("section", None, "tp"),
    )

    return jax.shard_map(shards, mesh=mesh, in_specs=in_specs, out_specs=out_specs, check_vma=False)
```

time: 196 us -> 134 us (0.68)
  the two profiles are of different devices: /device:TPU:50 before, /device:TPU:1 now
where the time goes in v2:
time: 134 us
  Pallas kernels  67.9 us (51%)
  starting transfers between devices  31.8 us (24%)
  waiting for transfers between devices  27.9 us (21%)
  other arithmetic  3.94 us (3%)
    pallas_call x2, Pallas kernels, local(): pl.pallas_call(functools.partial(local_kernel, first_pair=first, heads=he...  30.9 us
    pallas_call x2, Pallas kernels, inter(): pl.pallas_call(functools.partial(inter_kernel, first_pair=first, heads=he...  15.3 us
    all_to_all x1, starting transfers between devices, shards(): lax.all_to_all(pay, 'ctx', split_axis=0, concat_axis=0, tiled=True)  10.2 us
    all_to_all x1, waiting for transfers between devices, shards(): lax.all_to_all(scanned, 'ctx', split_axis=0, concat_axis=0, tiled=True)  10.1 us
    all_to_all x1, waiting for transfers between devices, shards(): lax.all_to_all(pay, 'ctx', split_axis=0, concat_axis=0, tiled=True)  10.1 us
    pallas_call x1, Pallas kernels, shards(): pl.pallas_call(functools.partial(prep_kernel, steps_per_group=steps_per_g...  9.52 us
    ppermute x2, waiting for transfers between devices, shards(): ups.append(lax.ppermute(up, 'section', route))  7.75 us
    pallas_call x1, Pallas kernels, shards(): pl.pallas_call(functools.partial(vectors_kernel, groups=groups, places=pl...  7.59 us
  transfers between devices with their start and end apart: 8, of which 3 were waited for; matrix products, arithmetic and copies ran while one was open for 4% of the time, Pallas kernels for 29%

profile of v2, /device:TPU:1, one launch (start us, length us, event | category | flops | bytes accessed | tf_op | source)
XLA Modules:
  0.0 133.6 jit_solution(1822713514870290887)
XLA Ops:
  0.6 9.5 %prep.1 = (bf16[16,264,128]{2,1,0:T(8,128)(2,1)}, bf16[16,128,128]{2,1,0:T(8,128)(2,1)}, bf16[512,192]{1,0:T(8,128)(2,1)}, f32[4,64,128]{2,1,0:T(8,128)}, bf16[2...) custom-call(bf16[512,2048]{1,0:T(8,128)(2,1)} %bitcast.16, bf16[512,2048]{1,0:T(8,128)(2,1)} %bitcast.19, ...), custom_call_target="tpu_custom_call" | custom-call | tf_op jit(solution)/shard_map/prep/pallas_call | solution.py:412
  10.2 10.2 %all-to-all-start = ((bf16[16,264,128]{2,1,0:T(8,128)(2,1)}), bf16[16,264,128]{2,1,0:T(8,128)(2,1)}, u32[]{:S(2)}, u32[]{:S(2)}) async-start(bf16[16,264,128]{2,1,0:T(8,128)(2,1)} %get-tuple-element.65.pay_ref), calls=%async_computation | async-start | bytes 2162688 | tf_op jit(solution)/shard_map/all_to_all | solution.py:511
  20.4 0.1 broadcast_in_dim.20
  20.4 0.7 broadcast_in_dim.21.skip_ref
  21.1 15.4 %local.2 = (f32[8,512,128]{2,1,0:T(8,128)}, f32[512,128]{1,0:T(8,128)}, f32[512,256]{1,0:T(8,128)}, f32[8,128]{1,0:T(8,128)}, bf16[8,512,256]{2,1,0:T(8,128)(2,1...) custom-call(bf16[512,2048]{1,0:T(8,128)(2,1)} %bitcast.17, bf16[512,2048]{1,0:T(8,128)(2,1)} %bitcast.20, ...), custom_call_target="tpu_custom_call" | custom-call | flops 20000000000 | bytes 67108864 | tf_op jit(solution)/shard_map/local/pallas_call | solution.py:461
  36.5 10.1 %all-to-all-done.in_ref = bf16[16,264,128]{2,1,0:T(8,128)(2,1)} async-done(((bf16[16,264,128]{2,1,0:T(8,128)(2,1)}), bf16[16,264,128]{2,1,0:T(8,128)(2,1)}, u32[]{:S(2)}, u32[]{:S(2)}) %all-to-all-start) | async-done | bytes 1081376 | tf_op jit(solution)/shard_map/all_to_all | solution.py:511
  46.6 2.4 %scan.1 = bf16[16,256,128]{2,1,0:T(8,128)(2,1)} custom-call(bf16[16,264,128]{2,1,0:T(8,128)(2,1)} %all-to-all-done.in_ref), custom_call_target="tpu_custom_call" | custom-call | tf_op jit(solution)/shard_map/scan/pallas_call | solution.py:514
  49.1 6.2 %all-to-all-start.1 = ((bf16[16,256,128]{2,1,0:T(8,128)(2,1)}), bf16[16,256,128]{2,1,0:T(8,128)(2,1)}, u32[]{:S(2)}, u32[]{:S(2)}) async-start(bf16[16,256,128]{2,1,0:T(8,128)(2,1)} %scan.1), calls=%async_computation.1 | async-start | bytes 2097152 | tf_op jit(solution)/shard_map/all_to_all | solution.py:524
  55.3 15.5 %local.3 = (f32[8,512,128]{2,1,0:T(8,128)}, f32[512,128]{1,0:T(8,128)}, f32[512,256]{1,0:T(8,128)}, f32[8,128]{1,0:T(8,128)}, bf16[8,512,256]{2,1,0:T(8,128)(2,1...) custom-call(bf16[512,2048]{1,0:T(8,128)(2,1)} %bitcast.18, bf16[512,2048]{1,0:T(8,128)(2,1)} %bitcast.21, ...), custom_call_target="tpu_custom_call" | custom-call | flops 20000000000 | bytes 67108864 | tf_op jit(solution)/shard_map/local/pallas_call | solution.py:461
  70.8 10.1 %all-to-all-done.1.st_ref.refs_2_.refs_6_ = bf16[16,256,128]{2,1,0:T(8,128)(2,1)} async-done(((bf16[16,256,128]{2,1,0:T(8,128)(2,1)}), bf16[16,256,128]{2,1,0:T(8,128)(2,1)}, u32[]{:S(2)}, u32[]{:S(2)}) %all-to-all-start.1) | async-done | bytes 1048608 | tf_op jit(solution)/shard_map/all_to_all | solution.py:524
  80.9 7.6 %inter.2 = (bf16[512,1024]{1,0:T(8,128)(2,1)}, f32[32,512]{1,0:T(8,128)}, f32[1,8,128]{2,1,0:T(8,128)}) custom-call(bf16[8,512,256]{2,1,0:T(8,128)(2,1)} %get-tuple-element.94.pushed_ref.refs_0_, bf16[8,512,256]{2,1,0:T(8,128)(2,1)} %get-tuple-element.95.drawn_ref.refs_1_, f32[8,512,128]{2,1,0:T(8,128)} %get-tuple-element.96.tail_ref, ...), custom_call_target="tpu_custom_call" | custom-call | flops 4000000000 | bytes 16777216 | tf_op jit(solution)/shard_map/inter/pallas_call | solution.py:492
  88.5 7.7 %inter.3 = (bf16[512,1024]{1,0:T(8,128)(2,1)}, f32[32,512]{1,0:T(8,128)}, f32[16,8,128]{2,1,0:T(8,128)}) custom-call(bf16[8,512,256]{2,1,0:T(8,128)(2,1)} %get-tuple-element.103.pushed_ref.refs_4_, bf16[8,512,256]{2,1,0:T(8,128)(2,1)} %get-tuple-element.104.drawn_ref.refs_5_, f32[8,512,128]{2,1,0:T(8,128)} %get-tuple-element.105.tail_ref, ...), custom_call_target="tpu_custom_call" | custom-call | flops 4000000000 | bytes 16777216 | tf_op jit(solution)/shard_map/inter/pallas_call | solution.py:492
  96.2 4.5 %collective-permute-start.1 = (bf16[512,1024]{1,0:T(8,128)(2,1)}, bf16[512,1024]{1,0:T(8,128)(2,1)}, u32[]{:S(2)}, u32[]{:S(2)}) collective-permute-start(bf16[512,1024]{1,0:T(8,128)(2,1)} %get-tuple-element.111), channel_id=1, source_target_pairs={{64,0},{128,64},{192,128},{65,1},{129,65},{193,129},{66,2},{130,66... | collective-permute-start | bytes 3145736 | tf_op jit(solution)/shard_map/ppermute | solution.py:533
  100.7 1.9 %collective-permute-start = (bf16[512,1024]{1,0:T(8,128)(2,1)}, bf16[512,1024]{1,0:T(8,128)(2,1)}, u32[]{:S(2)}, u32[]{:S(2)}) collective-permute-start(bf16[512,1024]{1,0:T(8,128)(2,1)} %get-tuple-element.102), channel_id=1, source_target_pairs={{64,0},{128,64},{192,128},{65,1},{129,65},{193,129},{66,2},{130,66... | collective-permute-start | bytes 3145736 | tf_op jit(solution)/shard_map/ppermute | solution.py:533
  102.6 4.2 %all-to-all-start.2 = ((f32[16,8,128]{2,1,0:T(8,128)}), f32[16,8,128]{2,1,0:T(8,128)}, u32[]{:S(2)}, u32[]{:S(2)}) async-start(f32[16,8,128]{2,1,0:T(8,128)} %get-tuple-element.112), calls=%async_computation.2 | async-start | bytes 131072 | tf_op jit(solution)/shard_map/all_to_all | solution.py:535
  106.8 7.6 %vectors.1 = (bf16[128,512]{1,0:T(8,128)(2,1)}, bf16[128,512]{1,0:T(8,128)(2,1)}, bf16[128,512]{1,0:T(8,128)(2,1)}, bf16[128,512]{1,0:T(8,128)(2,1)}) custom-call(s32[1]{0:T(128)} %bitcast.8.me_ref, bf16[8,512,256]{2,1,0:T(8,128)(2,1)} %get-tuple-element.94.pushed_ref.refs_0_, bf16[8,512,256]{2,1,0:T(8,128)(2,1)} %get-tuple-element.95.drawn_ref.refs_1_, ...), custom_call_target="tpu_custom_call" | custom-call | flops 4000000000 | bytes 16777216 | tf_op jit(solution)/shard_map/vectors/pallas_call | solution.py:541
  114.3 1.2 collective-permute-start.2
  115.6 2.4 %collective-permute-start.3 = (bf16[128,512]{1,0:T(8,128)(2,1)}, bf16[128,512]{1,0:T(8,128)(2,1)}, u32[]{:S(2)}, u32[]{:S(2)}) collective-permute-start(bf16[128,512]{1,0:T(8,128)(2,1)} %get-tuple-element.117), channel_id=1, source_target_pairs={{0,2},{1,3},{2,0},{3,1},{4,6},{5,7},{6,4},{7,5},{8,10},{9,11},{10,... | collective-permute-start | bytes 393224 | tf_op jit(solution)/shard_map/ppermute | solution.py:560
  118.0 1.2 collective-permute-start.4
  119.2 0.9 reduce_sum.9
  120.0 7.7 %collective-permute-done = bf16[512,1024]{1,0:T(8,128)(2,1)} collective-permute-done((bf16[512,1024]{1,0:T(8,128)(2,1)}, bf16[512,1024]{1,0:T(8,128)(2,1)}, u32[]{:S(2)}, u32[]{:S(2)}) %collective-permute-start) | collective-permute-done | bytes 1048608 | tf_op jit(solution)/shard_map/ppermute | solution.py:533
  127.8 3.1 %pad_maximum_fusion = bf16[512,2048]{1,0:T(8,128)(2,1)} fusion(bf16[512,1024]{1,0:T(8,128)(2,1)} %collective-permute-done.1, bf16[512,1024]{1,0:T(8,128)(2,1)} %collective-permute-done), kind=kLoop, calls=%fused_computation | loop fusion | flops 4194304 | bytes 4194304 | tf_op jit(solution)/shard_map/concatenate | solution.py:538
  130.9 0.6 copy.12
  131.4 2.1 %rows.1 = f32[128,2048]{1,0:T(8,128)} custom-call(s32[1]{0:T(128)} %bitcast.8.me_ref, bf16[128,512]{1,0:T(8,128)(2,1)} %get-tuple-element.121.refs_0_, bf16[128,512]{1,0:T(8,128)(2,1)} %collective-permute-done.2.refs_1_, bf16[128,512]{1,0:T(8,128)(2,1)} %collective-permute-done.3.refs_2_, bf16[128,512]{1,0:T(8,128)(2,1)} %collective-permute-done.4.refs_3_), custom_call_target="tpu_custom_call" | custom-call | tf_op jit(solution)/shard_map/rows/pallas_call | solution.py:564
  (8 shorter events, 0.0 us)
Async XLA Ops:
  10.2 10.2 %copy-start = (f32[1,32]{1,0:T(1,128)S(1)}, f32[1,32]{1,0:T(1,128)}, u32[]{:S(2)}) copy-start(f32[1,32]{1,0:T(1,128)} %param.14) | copy-start | bytes 388
  10.2 36.5 %all-to-all-start = ((bf16[16,264,128]{2,1,0:T(8,128)(2,1)}), bf16[16,264,128]{2,1,0:T(8,128)(2,1)}, u32[]{:S(2)}, u32[]{:S(2)}) async-start(bf16[16,264,128]{2,1,0:T(8,128)(2,1)} %get-tuple-element.65.pay_ref), calls=%async_computation | async-start | bytes 2162688 | tf_op jit(solution)/shard_map/all_to_all | solution.py:511
  49.1 31.8 %all-to-all-start.1 = ((bf16[16,256,128]{2,1,0:T(8,128)(2,1)}), bf16[16,256,128]{2,1,0:T(8,128)(2,1)}, u32[]{:S(2)}, u32[]{:S(2)}) async-start(bf16[16,256,128]{2,1,0:T(8,128)(2,1)} %scan.1), calls=%async_computation.1 | async-start | bytes 2097152 | tf_op jit(solution)/shard_map/all_to_all | solution.py:524
  96.2 23.9 %collective-permute-start.1 = (bf16[512,1024]{1,0:T(8,128)(2,1)}, bf16[512,1024]{1,0:T(8,128)(2,1)}, u32[]{:S(2)}, u32[]{:S(2)}) collective-permute-start(bf16[512,1024]{1,0:T(8,128)(2,1)} %get-tuple-element.111), channel_id=1, source_target_pairs={{64,0},{128,64},{192,128},{65,1},{129,65},{193,129},{66,2},{130,66... | collective-permute-start | bytes 3145736 | tf_op jit(solution)/shard_map/ppermute | solution.py:533
  100.7 27.1 %collective-permute-start = (bf16[512,1024]{1,0:T(8,128)(2,1)}, bf16[512,1024]{1,0:T(8,128)(2,1)}, u32[]{:S(2)}, u32[]{:S(2)}) collective-permute-start(bf16[512,1024]{1,0:T(8,128)(2,1)} %get-tuple-element.102), channel_id=1, source_target_pairs={{64,0},{128,64},{192,128},{65,1},{129,65},{193,129},{66,2},{130,66... | collective-permute-start | bytes 3145736 | tf_op jit(solution)/shard_map/ppermute | solution.py:533
  102.6 16.6 %all-to-all-start.2 = ((f32[16,8,128]{2,1,0:T(8,128)}), f32[16,8,128]{2,1,0:T(8,128)}, u32[]{:S(2)}, u32[]{:S(2)}) async-start(f32[16,8,128]{2,1,0:T(8,128)} %get-tuple-element.112), calls=%async_computation.2 | async-start | bytes 131072 | tf_op jit(solution)/shard_map/all_to_all | solution.py:535
  114.3 16.5 %collective-permute-start.2 = (bf16[128,512]{1,0:T(8,128)(2,1)}, bf16[128,512]{1,0:T(8,128)(2,1)}, u32[]{:S(2)}, u32[]{:S(2)}) collective-permute-start(bf16[128,512]{1,0:T(8,128)(2,1)} %get-tuple-element.116), channel_id=1, source_target_pairs={{0,1},{1,2},{2,3},{3,0},{4,5},{5,6},{6,7},{7,4},{8,9},{9,10},{10,1... | collective-permute-start | bytes 393224 | tf_op jit(solution)/shard_map/ppermute | solution.py:560
  115.6 15.3 %collective-permute-start.3 = (bf16[128,512]{1,0:T(8,128)(2,1)}, bf16[128,512]{1,0:T(8,128)(2,1)}, u32[]{:S(2)}, u32[]{:S(2)}) collective-permute-start(bf16[128,512]{1,0:T(8,128)(2,1)} %get-tuple-element.117), channel_id=1, source_target_pairs={{0,2},{1,3},{2,0},{3,1},{4,6},{5,7},{6,4},{7,5},{8,10},{9,11},{10,... | collective-permute-start | bytes 393224 | tf_op jit(solution)/shard_map/ppermute | solution.py:560
  118.0 12.9 %collective-permute-start.4 = (bf16[128,512]{1,0:T(8,128)(2,1)}, bf16[128,512]{1,0:T(8,128)(2,1)}, u32[]{:S(2)}, u32[]{:S(2)}) collective-permute-start(bf16[128,512]{1,0:T(8,128)(2,1)} %get-tuple-element.118), channel_id=1, source_target_pairs={{0,3},{1,0},{2,1},{3,2},{4,7},{5,4},{6,5},{7,6},{8,11},{9,8},{10,9... | collective-permute-start | bytes 393224 | tf_op jit(solution)/shard_map/ppermute | solution.py:560

commit v3 on v2

--- a/solution.py
+++ b/solution.py
@@ -147,26 +147,28 @@
         low_ref[k] = state_lo[:, lanes]
 
 
-def scan_kernel(in_ref, out_ref):
+def scan_kernel(in_ref, mark_ref, out_ref):
     places = in_ref.shape[0]
 
-    def carry(c):
-        tail = in_ref[c, 2 * STATE :].astype(F32)
-        return tail[0:1] + tail[1:2]
-
-    state = jnp.zeros((STATE, LANES), F32)
-    for c in range(places):
-        out_ref[c, :STATE] = state.astype(BF16)
-        state = carry(c) * state + in_ref[c, :STATE].astype(F32)
-    grad = jnp.zeros((STATE, LANES), F32)
-    for c in reversed(range(places)):
-        out_ref[c, STATE:] = grad.astype(BF16)
-        grad = carry(c) * grad + in_ref[c, STATE : 2 * STATE].astype(F32)
+    def run(order):
+        total = jnp.zeros((STATE, LANES), F32)
+        for c in order:
+            out_ref[c] = total.astype(BF16)
+            mark = mark_ref[c].astype(F32)
+            total = (mark[0:1] + mark[1:2]) * total + in_ref[c].astype(F32)
+
+    @pl.when(pl.program_id(0) == 0)
+    def _():
+        run(range(places))
+
+    @pl.when(pl.program_id(0) == 1)
+    def _():
+        run(reversed(range(places)))
 
 
 def local_kernel(
     x_ref, dy_ref, w_ref, r_ref, wt_ref, rt_ref, cs_ref, ct_ref, skip_ref,
-    dxi_ref, vp_ref, dwr_ref, gsk_ref, pushed_ref, drawn_ref, tail_ref,
+    dxi_ref, vp_ref, dwr_ref, gsk_ref, pushed_ref, tail_ref,
     sc_ref, sct_ref, dsc_ref, states_ref, base_ref, sum_base_ref, *, first_pair, heads
 ):
     place = pl.program_id(0)
@@ -253,7 +255,6 @@
         skip_sum = skip_sum + jnp.sum(xf * dyf, axis=0, keepdims=True)
         pushed_ref[0, rows] = jnp.concatenate(split2(dyf * jnp.exp(before[c] + cl[rows])), 1)
         tail = jnp.exp((before[chunks] - before[c]) - ll[rows])
-        drawn_ref[0, rows] = jnp.concatenate(split2(xf * tail), 1)
         tail_ref[0, rows] = tail
     gsk_ref[...] += head_sum(jnp.broadcast_to(skip_sum, (gsk_ref.shape[0], LANES)), pick_push)
 
@@ -270,37 +271,50 @@
 
 
 def inter_kernel(
-    pushed_ref, drawn_ref, tail_ref, w_ref, r_ref, pay_ref, low_ref, st_ref, dxi_ref, vp_in_ref,
-    gsk_ref, delta_ref, rate_ref, bias_ref, *refs, first_pair, heads, copies
+    me_ref, pushed_ref, tail_ref, x_ref, w_ref, r_ref, pay_ref, low_ref, st_ref, dxi_ref, vp_in_ref, dwr_in_ref,
+    gsk_ref, delta_ref, rate_ref, bias_ref, *refs, first_pair, heads, copies, places
 ):
-    *refs, up_ref, gd_ref, prm_ref, vp_ref, sum_base_ref = refs
+    *refs, vp_ref, sum_ref, sum_base_ref = refs
+    if first_pair:
+        gd_in_ref, prm_in_ref, rows_in_ref, *refs = refs
+    up_ref, gd_ref, prm_ref, *rows_refs = refs
     place = pl.program_id(0)
     batch, length = pushed_ref.shape[:2]
 
     @pl.when(place == 0)
     def _():
         vp_ref[...] = vp_in_ref[...]
+        sum_ref[...] = dwr_in_ref[...]
         fill_sum_base(sum_base_ref)
 
     sums = None
+    drawn_parts, pushed_parts, grads, states = [], [], [], []
     for k in range(batch):
         pair = first_pair + place * batch + k
+        lanes = slice(k * LANES, (k + 1) * LANES)
         state, grad = st_ref[k, :STATE], st_ref[k, STATE:]
         mark = pay_ref[k, 2 * STATE :].astype(F32)
         own = pay_ref[k, :STATE].astype(F32) + low_ref[k].astype(F32)
         ending = own + (mark[0:1] + mark[1:2]) * state.astype(F32)
         edge = jnp.sum(ending * grad.astype(F32), axis=0, keepdims=True)
-        pushed, drawn = pushed_ref[k], drawn_ref[k]
+        pushed, tail = pushed_ref[k], tail_ref[k]
+        drawn = x_ref[:, lanes].astype(F32) * tail
         y = mm(r_ref[...], state)
         dx = mm(w_ref[...], grad)
-        pulled = (drawn[:, :LANES].astype(F32) + drawn[:, LANES:].astype(F32)) * dx
+        pulled = drawn * dx
         push = (pushed[:, :LANES].astype(F32) + pushed[:, LANES:].astype(F32)) * y - pulled
         push = push + jnp.where(iota((length, LANES), 0) == length - 1, edge, 0.0)
         found = head_sum(push, sum_pick(sum_base_ref, 2 * pair))
         found = found + head_sum(pulled, sum_pick(sum_base_ref, 2 * heads + 2 * pair))
         sums = found if sums is None else sums + found
-        up_ref[:, k * LANES : (k + 1) * LANES] = (dxi_ref[k] + tail_ref[k] * dx).astype(BF16)
+        up_ref[:, lanes] = (dxi_ref[k] + tail * dx).astype(BF16)
+        drawn_parts += split2(drawn)
+        pushed_parts.append(pushed)
+        grads += [grad, grad]
+        states += [state, state]
     vp_ref[...] += sums
+    sum_ref[:, :STATE] += mm_nt(jnp.concatenate(drawn_parts, 1), jnp.concatenate(grads, 1))
+    sum_ref[:, STATE:] += mm_nt(jnp.concatenate(pushed_parts, 1), jnp.concatenate(states, 1))
 
     @pl.when(place == pl.num_programs(0) - 1)
     def _():
@@ -324,7 +338,7 @@
             rate_sum = rate_sum - rate * later * step
             bias_sum = bias_sum + grad_delta
             if first_pair:
-                grad_delta = grad_delta + refs[0][:, rows]
+                grad_delta = grad_delta + gd_in_ref[:, rows]
             gd_ref[:, rows] = grad_delta
         lane = iota((heads, LANES), 1)
         rate_sum = jnp.sum(rate_sum, axis=1, keepdims=True)
@@ -333,43 +347,24 @@
         both = jnp.concatenate([both, jnp.zeros((LANES - heads, LANES), F32)], 0).T[:8]
         sums = jnp.where(iota((8, LANES), 0) == 2, gsk_ref[...], both)
         if first_pair:
-            sums = sums + refs[1][0]
+            sums = sums + prm_in_ref[0]
         for k in range(copies):
             prm_ref[k] = sums
-
-
-def vectors_kernel(me_ref, *refs, groups, places):
-    out_refs, sum_ref = refs[4 * groups : -1], refs[-1]
-    place = pl.program_id(0)
-    length = refs[0].shape[1]
-    for g in range(groups):
-        pushed_ref, drawn_ref, st_ref, dwr_ref = refs[4 * g : 4 * g + 4]
-        cols = slice(g * 2 * STATE, (g + 1) * 2 * STATE)
-
-        @pl.when(place == 0)
-        def _():
-            sum_ref[:, cols] = dwr_ref[...]
-
-        batch = pushed_ref.shape[0]
-        half = g * 2 * STATE + STATE
-        for ref, cols, part in (
-            (drawn_ref, slice(half - STATE, half), slice(STATE, 2 * STATE)),
-            (pushed_ref, slice(half, half + STATE), slice(0, STATE)),
-        ):
-            left = jnp.concatenate([ref[k] for k in range(batch)], axis=1)
-            right = jnp.concatenate([st_ref[k, part] for k in range(batch) for _ in range(2)], axis=1)
-            sum_ref[:, cols] += mm_nt(left, right)
-
-    @pl.when(place == pl.num_programs(0) - 1)
-    def _():
-        rows = length // places
-        for hop in range(places):
-            start = pl.multiple_of(lax.rem(me_ref[0] + hop, places) * rows, rows)
-            out_refs[hop][...] = sum_ref[pl.ds(start, rows), :].astype(BF16)
-
-
-def rows_kernel(me_ref, *refs):
-    *in_refs, out_ref = refs
+        rows = length // len(rows_refs)
+        for hop, ref in enumerate(rows_refs):
+            start = pl.multiple_of(lax.rem(me_ref[0] + hop, places) * rows, rows) if len(rows_refs) > 1 else 0
+            if first_pair:
+                ref[:, : -2 * STATE] = rows_in_ref[pl.ds(start, rows), :]
+            ref[:, -2 * STATE :] = sum_ref[pl.ds(start, rows), :].astype(BF16)
+
+
+def first_kernel(in_ref, out_ref):
+    out_ref[...] = in_ref[...]
+
+
+def last_kernel(me_ref, buffer_ref, up_ref, *refs):
+    *in_refs, all_ref, out_ref = refs
+    all_ref[...] = up_ref[...]
     places = len(in_refs)
     width = in_refs[0].shape[1]
     for hop, ref in enumerate(in_refs):
@@ -467,7 +462,7 @@
                 pl.BlockSpec((1, LANES), lambda p: (0, first + p)),
             ],
             out_specs=[
-                own_col, whole(length, LANES), whole(length, 2 * STATE), whole(8, LANES), own_two, own_two, own_col
+                own_col, whole(length, LANES), whole(length, 2 * STATE), whole(8, LANES), own_two, own_col
             ],
             out_shape=[
                 sds((per_group, length, LANES), F32),
@@ -475,7 +470,6 @@
                 sds((length, 2 * STATE), F32),
                 sds((8, LANES), F32),
                 sds((per_group, length, 2 * LANES), BF16),
-                sds((per_group, length, 2 * LANES), BF16),
                 sds((per_group, length, LANES), F32),
             ],
             scratch_shapes=[pltpu.VMEM((length // CHUNK, CHUNK, CHUNK), F32)] * 4
@@ -487,39 +481,55 @@
 
     def inter(g, edges, own, carried):
         first, _, grp_g, _ = group_specs(g)
-        dxi, vp, _, gsk, pushed, drawn, tail = own
-        mine = copies if g == groups - 1 else 1
+        dxi, vp, dwr, gsk, pushed, tail = own
+        final = g == groups - 1
+        mine = copies if final else 1
+        row_width = 2 * STATE * (g + 1)
+        row_shapes = [(length // places, row_width)] * places if final else [(length, row_width)]
         return pl.pallas_call(
-            functools.partial(inter_kernel, first_pair=first, heads=heads, copies=mine),
+            functools.partial(inter_kernel, first_pair=first, heads=heads, copies=mine, places=places),
             grid=(trips,),
             in_specs=[
-                many(length, 2 * LANES), many(length, 2 * LANES), many(length, LANES), grp_g, grp_g,
+                pl.BlockSpec(memory_space=pltpu.SMEM),
+                many(length, 2 * LANES), many(length, LANES),
+                pl.BlockSpec((length, batch * LANES), lambda p: (0, g * trips + p)), grp_g, grp_g,
                 many_of(g, pay_rows, LANES), many_of(g, STATE, LANES), many_of(g, 2 * STATE, LANES),
-                many(length, LANES), whole(length, LANES), whole(8, LANES),
+                many(length, LANES), whole(length, LANES), whole(length, 2 * STATE), whole(8, LANES),
                 whole(heads, length), whole(1, heads), whole(1, heads), *[whole(*a.shape) for a in carried],
             ],
             out_specs=[
-                pl.BlockSpec((length, batch * LANES), lambda p: (0, p)), whole(heads, length), whole(mine, 8, LANES)
-            ],
-            out_shape=[sds((length, group_width), BF16), sds((heads, length), F32), sds((mine, 8, LANES), F32)],
-            scratch_shapes=[pltpu.VMEM((length, LANES), F32), pltpu.VMEM((2 * LANES, LANES), jnp.int32)],
+                pl.BlockSpec((length, batch * LANES), lambda p: (0, p)), whole(heads, length), whole(mine, 8, LANES),
+                *[whole(*shape) for shape in row_shapes],
+            ],
+            out_shape=[
+                sds((length, group_width), BF16), sds((heads, length), F32), sds((mine, 8, LANES), F32),
+                *[sds(shape, BF16) for shape in row_shapes],
+            ],
+            scratch_shapes=[
+                pltpu.VMEM((length, LANES), F32),
+                pltpu.VMEM((length, 2 * STATE), F32),
+                pltpu.VMEM((2 * LANES, LANES), jnp.int32),
+            ],
             compiler_params=params(),
             cost_estimate=cost(4 * 10**9, 16 << 20),
             name="inter",
-        )(pushed, drawn, tail, w, r, pay, low, edges, dxi, vp, gsk, delta, log_rates, delta_bias, *carried)
+        )(me, pushed, tail, x, w, r, pay, low, edges, dxi, vp, dwr, gsk, delta, log_rates, delta_bias, *carried)
 
     arrived = lax.all_to_all(pay, "ctx", split_axis=0, concat_axis=0, tiled=True)
     own = [local(0, cs)]
     arrived, own[0] = lax.optimization_barrier((arrived, own[0]))
     scanned = pl.pallas_call(
         scan_kernel,
-        in_specs=[whole(pairs, pay_rows, LANES)],
-        out_specs=whole(pairs, 2 * STATE, LANES),
+        in_specs=[
+            pl.BlockSpec((pairs, STATE, LANES), lambda i: (0, i, 0)),
+            pl.BlockSpec((pairs, TAIL, LANES), lambda i: (0, 2 * STATE // TAIL, 0)),
+        ],
+        out_specs=pl.BlockSpec((pairs, STATE, LANES), lambda i: (0, i, 0)),
         out_shape=sds((pairs, 2 * STATE, LANES), BF16),
         compiler_params=params(),
-        grid=(1,),
+        grid=(2,),
         name="scan",
-    )(arrived)
+    )(arrived, arrived)
     scanned, cs_later = lax.optimization_barrier((scanned, cs))
     edges = lax.all_to_all(scanned, "ctx", split_axis=0, concat_axis=0, tiled=True)
     own += [local(g, cs_later) for g in range(1, groups)]
@@ -531,45 +541,40 @@
     for g in range(groups):
         up, *carried = inter(g, edges, own[g], carried)
         ups.append(lax.ppermute(up, "section", route))
-    grad_delta, sums = carried
+    grad_delta, sums, *row_blocks = carried
     everyone = lax.all_to_all(sums, "ctx", split_axis=0, concat_axis=0, tiled=True)
-
+    got = row_blocks[:1]
+    for hop in range(1, places):
+        got.append(lax.ppermute(row_blocks[hop], "tp", [(i, (i + hop) % places) for i in range(places)]))
     param_sums = jnp.sum(everyone, axis=0)[:3, :heads]
-    upstream = jnp.concatenate(ups, axis=1)
-    row_shape = (length // places, groups * 2 * STATE)
-    pieces = [a for g in range(groups) for a in (own[g][4], own[g][5], edges, own[g][2])]
-    row_blocks = pl.pallas_call(
-        functools.partial(vectors_kernel, groups=groups, places=places),
-        grid=(trips,),
-        in_specs=[pl.BlockSpec(memory_space=pltpu.SMEM)]
-        + [
-            spec
-            for g in range(groups)
-            for spec in (
-                many(length, 2 * LANES), many(length, 2 * LANES), many_of(g, 2 * STATE, LANES), whole(length, 2 * STATE)
-            )
+    before = width - group_width
+    start = jnp.concatenate(ups[:-1], axis=1) if groups > 2 else ups[0]
+    buffer = pl.pallas_call(
+        first_kernel,
+        grid=(1,),
+        in_specs=[whole(length, before)],
+        out_specs=whole(length, before),
+        out_shape=sds((length, width), BF16),
+        compiler_params=params(),
+        cost_estimate=cost(10**6, 2 << 20),
+        name="first",
+    )(start)
+    row_shape = row_blocks[0].shape
+    upstream, vector_rows = pl.pallas_call(
+        last_kernel,
+        grid=(1,),
+        in_specs=[
+            pl.BlockSpec(memory_space=pltpu.SMEM), pl.BlockSpec(memory_space=pl.ANY), whole(length, group_width)
+        ]
+        + [whole(*row_shape)] * places,
+        out_specs=[
+            pl.BlockSpec((length, group_width), lambda i: (0, groups - 1)), whole(row_shape[0], row_shape[1] * places)
         ],
-        out_specs=[whole(*row_shape)] * places,
-        out_shape=[sds(row_shape, BF16)] * places,
-        scratch_shapes=[pltpu.VMEM((length, row_shape[1]), F32)],
+        out_shape=[sds((length, width), BF16), sds((row_shape[0], row_shape[1] * places), F32)],
+        input_output_aliases={1: 0},
         compiler_params=params(),
-        cost_estimate=cost(4 * 10**9, 16 << 20),
-        name="vectors",
-    )(me, *pieces)
-    got = [
-        lax.ppermute(part, "tp", [(i, (i + hop) % places) for i in range(places)]) if hop else part
-        for hop, part in enumerate(row_blocks)
-    ]
-    upstream, param_sums, got = lax.optimization_barrier((upstream, param_sums, got))
-    vector_rows = pl.pallas_call(
-        rows_kernel,
-        grid=(1,),
-        in_specs=[pl.BlockSpec(memory_space=pltpu.SMEM)] + [whole(*row_shape)] * places,
-        out_specs=whole(row_shape[0], row_shape[1] * places),
-        out_shape=sds((row_shape[0], row_shape[1] * places), F32),
-        compiler_params=params(),
-        name="rows",
-    )(me, *got)
+        name="last",
+    )(me, buffer, ups[-1], *got)
     return upstream[None], grad_delta.T[None], vector_rows[None], param_sums[None]
 
 

time: 134 us -> 125 us (0.933)
  the two profiles are of different devices: /device:TPU:1 before, /device:TPU:50 now
where the time goes in v3:
time: 125 us; the launch traced here: 124 us
  Pallas kernels  64.6 us (52%)
  starting transfers between devices  29.7 us (24%)
  waiting for transfers between devices  27.3 us (22%)
  local copies, waits for them, and re-layouts  1.33 us (1%)
    pallas_call x2, Pallas kernels, local(): pl.pallas_call(functools.partial(local_kernel, first_pair=first, heads=he...  30.6 us
    pallas_call x2, Pallas kernels, inter(): pl.pallas_call(functools.partial(inter_kernel, first_pair=first, heads=he...  17.2 us
    all_to_all x1, waiting for transfers between devices, shards(): lax.all_to_all(scanned, 'ctx', split_axis=0, concat_axis=0, tiled=True)  11.2 us
    all_to_all x1, waiting for transfers between devices, shards(): lax.all_to_all(pay, 'ctx', split_axis=0, concat_axis=0, tiled=True)  11 us
    pallas_call x1, Pallas kernels, shards(): pl.pallas_call(functools.partial(prep_kernel, steps_per_group=steps_per_g...  9.51 us
    all_to_all x1, starting transfers between devices, shards(): lax.all_to_all(pay, 'ctx', split_axis=0, concat_axis=0, tiled=True)  9.32 us
    all_to_all x1, starting transfers between devices, shards(): lax.all_to_all(sums, 'ctx', split_axis=0, concat_axis=0, tiled=True)  5.88 us
    all_to_all x1, starting transfers between devices, shards(): lax.all_to_all(scanned, 'ctx', split_axis=0, concat_axis=0, tiled=True)  5.24 us
  transfers between devices with their start and end apart: 8, of which 3 were waited for; matrix products, arithmetic and copies ran while one was open for 1% of the time, Pallas kernels for 34%

profile of v3, /device:TPU:50, one launch (start us, length us, event | category | flops | bytes accessed | tf_op | source)
XLA Modules:
  0.0 123.7 jit_solution(12849157996215228359)
XLA Ops:
  0.6 9.5 %prep.1 = (bf16[16,264,128]{2,1,0:T(8,128)(2,1)}, bf16[16,128,128]{2,1,0:T(8,128)(2,1)}, bf16[512,192]{1,0:T(8,128)(2,1)}, f32[4,64,128]{2,1,0:T(8,128)}, bf16[2...) custom-call(bf16[512,2048]{1,0:T(8,128)(2,1)} %bitcast.20, bf16[512,2048]{1,0:T(8,128)(2,1)} %bitcast.17, ...), custom_call_target="tpu_custom_call" | custom-call | tf_op jit(solution)/shard_map/prep/pallas_call | solution.py:407
  10.1 0.0 copy-start
  10.2 9.3 %all-to-all-start = ((bf16[16,264,128]{2,1,0:T(8,128)(2,1)}), bf16[16,264,128]{2,1,0:T(8,128)(2,1)}, u32[]{:S(2)}, u32[]{:S(2)}) async-start(bf16[16,264,128]{2,1,0:T(8,128)(2,1)} %get-tuple-element.57.pay_ref), calls=%async_computation | async-start | bytes 2162688 | tf_op jit(solution)/shard_map/all_to_all | solution.py:518
  19.5 0.1 broadcast_in_dim.21
  19.6 0.7 broadcast_in_dim.22.skip_ref
  20.2 15.3 %local.2 = (f32[8,512,128]{2,1,0:T(8,128)}, f32[512,128]{1,0:T(8,128)}, f32[512,256]{1,0:T(8,128)}, f32[8,128]{1,0:T(8,128)}, bf16[8,512,256]{2,1,0:T(8,128)(2,1)}, /*index=5*/f32[8,512,128]{2,1,0:T(8,128)}) custom-call(bf16[512,2048]{1,0:T(8,128)(2,1)} %bitcast.21, bf16[512,2048]{1,0:T(8,128)(2,1)} %bitcast.18, bf16[512,256]{1,0:T(8,128)(2,1)} %bitcast.26, ...), custom_call_target="tpu_custom_call" | custom-call | flops 20000000000 | bytes 67108864 | tf_op jit(solution)/shard_map/local/pallas_call | solution.py:456
  35.5 11.0 %all-to-all-done.in_ref.mark_ref = bf16[16,264,128]{2,1,0:T(8,128)(2,1)} async-done(((bf16[16,264,128]{2,1,0:T(8,128)(2,1)}), bf16[16,264,128]{2,1,0:T(8,128)(2,1)}, u32[]{:S(2)}, u32[]{:S(2)}) %all-to-all-start) | async-done | bytes 1081376 | tf_op jit(solution)/shard_map/all_to_all | solution.py:518
  46.5 2.1 %scan.1 = bf16[16,256,128]{2,1,0:T(8,128)(2,1)} custom-call(bf16[16,264,128]{2,1,0:T(8,128)(2,1)} %all-to-all-done.in_ref.mark_ref, bf16[16,264,128]{2,1,0:T(8,128)(2,1)} %all-to-all-done.in_ref.mark_ref), custom_call_target="tpu_custom_call" | custom-call | tf_op jit(solution)/shard_map/scan/pallas_call | solution.py:521
  48.7 5.2 %all-to-all-start.1 = ((bf16[16,256,128]{2,1,0:T(8,128)(2,1)}), bf16[16,256,128]{2,1,0:T(8,128)(2,1)}, u32[]{:S(2)}, u32[]{:S(2)}) async-start(bf16[16,256,128]{2,1,0:T(8,128)(2,1)} %scan.1), calls=%async_computation.1 | async-start | bytes 2097152 | tf_op jit(solution)/shard_map/all_to_all | solution.py:534
  53.9 15.3 %local.3 = (f32[8,512,128]{2,1,0:T(8,128)}, f32[512,128]{1,0:T(8,128)}, f32[512,256]{1,0:T(8,128)}, f32[8,128]{1,0:T(8,128)}, bf16[8,512,256]{2,1,0:T(8,128)(2,1)}, /*index=5*/f32[8,512,128]{2,1,0:T(8,128)}) custom-call(bf16[512,2048]{1,0:T(8,128)(2,1)} %bitcast.22, bf16[512,2048]{1,0:T(8,128)(2,1)} %bitcast.19, bf16[512,256]{1,0:T(8,128)(2,1)} %bitcast.27, ...), custom_call_target="tpu_custom_call" | custom-call | flops 20000000000 | bytes 67108864 | tf_op jit(solution)/shard_map/local/pallas_call | solution.py:456
  69.2 11.2 %all-to-all-done.1.st_ref = bf16[16,256,128]{2,1,0:T(8,128)(2,1)} async-done(((bf16[16,256,128]{2,1,0:T(8,128)(2,1)}), bf16[16,256,128]{2,1,0:T(8,128)(2,1)}, u32[]{:S(2)}, u32[]{:S(2)}) %all-to-all-start.1) | async-done | bytes 1048608 | tf_op jit(solution)/shard_map/all_to_all | solution.py:534
  80.4 8.5 %inter.2 = (bf16[512,1024]{1,0:T(8,128)(2,1)}, f32[32,512]{1,0:T(8,128)}, f32[1,8,128]{2,1,0:T(8,128)}, bf16[512,256]{1,0:T(8,128)(2,1)}) custom-call(s32[1]{0:T(128)} %bitcast.me_ref, bf16[8,512,256]{2,1,0:T(8,128)(2,1)} %get-tuple-element.83.pushed_ref, f32[8,512,128]{2,1,0:T(8,128)} %get-tuple-element.84.tail_ref, bf16[512,2048]{1,0:T(8,128)(2,1)} %bitcast.23, ...), custom_call_target="tpu_custom_call" | custom-call | flops 4000000000 | bytes 16777216 | tf_op jit(solution)/shard_map/inter/pallas_call | solution.py:489
  88.9 1.9 %collective-permute-start = (bf16[512,1024]{1,0:T(8,128)(2,1)}, bf16[512,1024]{1,0:T(8,128)(2,1)}, u32[]{:S(2)}, u32[]{:S(2)}) collective-permute-start(bf16[512,1024]{1,0:T(8,128)(2,1)} %get-tuple-element.91), channel_id=1, source_target_pairs={{64,0},{128,64},{192,128},{65,1},{129,65},{193,129},{66,2},{130,66... | collective-permute-start | bytes 3145736 | tf_op jit(solution)/shard_map/ppermute | solution.py:543
  90.9 8.7 %inter.3 = (bf16[512,1024]{1,0:T(8,128)(2,1)}, f32[32,512]{1,0:T(8,128)}, f32[16,8,128]{2,1,0:T(8,128)}, bf16[128,512]{1,0:T(8,128)(2,1)}, bf16[128,512]{1,0:T(8...) custom-call(s32[1]{0:T(128)} %bitcast.me_ref, bf16[8,512,256]{2,1,0:T(8,128)(2,1)} %get-tuple-element.92.pushed_ref, ...), custom_call_target="tpu_custom_call" | custom-call | flops 4000000000 | bytes 16777216 | tf_op jit(solution)/shard_map/inter/pallas_call | solution.py:489
  99.6 2.6 %collective-permute-start.1 = (bf16[512,1024]{1,0:T(8,128)(2,1)}, bf16[512,1024]{1,0:T(8,128)(2,1)}, u32[]{:S(2)}, u32[]{:S(2)}) collective-permute-start(bf16[512,1024]{1,0:T(8,128)(2,1)} %get-tuple-element.101), channel_id=1, source_target_pairs={{64,0},{128,64},{192,128},{65,1},{129,65},{193,129},{66,2},{130,66... | collective-permute-start | bytes 3145736 | tf_op jit(solution)/shard_map/ppermute | solution.py:543
  102.2 5.9 %all-to-all-start.2 = ((f32[16,8,128]{2,1,0:T(8,128)}), f32[16,8,128]{2,1,0:T(8,128)S(1)}, u32[]{:S(2)}, u32[]{:S(2)}) async-start(f32[16,8,128]{2,1,0:T(8,128)} %get-tuple-element.109), calls=%async_computation.2 | async-start | bytes 131072 | tf_op jit(solution)/shard_map/all_to_all | solution.py:545
  108.1 1.5 %collective-permute-start.2 = (bf16[128,512]{1,0:T(8,128)(2,1)}, bf16[128,512]{1,0:T(8,128)(2,1)}, u32[]{:S(2)}, u32[]{:S(2)}) collective-permute-start(bf16[128,512]{1,0:T(8,128)(2,1)} %get-tuple-element.103), channel_id=1, source_target_pairs={{0,1},{1,2},{2,3},{3,0},{4,5},{5,6},{6,7},{7,4},{8,9},{9,10},{10,1... | collective-permute-start | bytes 393224 | tf_op jit(solution)/shard_map/ppermute | solution.py:548
  109.6 1.1 collective-permute-start.3
  110.7 2.1 %collective-permute-start.4 = (bf16[128,512]{1,0:T(8,128)(2,1)}, bf16[128,512]{1,0:T(8,128)(2,1)}, u32[]{:S(2)}, u32[]{:S(2)}) collective-permute-start(bf16[128,512]{1,0:T(8,128)(2,1)} %get-tuple-element.105), channel_id=1, source_target_pairs={{0,3},{1,0},{2,1},{3,2},{4,7},{5,4},{6,5},{7,6},{8,11},{9,8},{10,9... | collective-permute-start | bytes 393224 | tf_op jit(solution)/shard_map/ppermute | solution.py:548
  112.9 5.1 %all-to-all-done.2 = f32[16,8,128]{2,1,0:T(8,128)S(1)} async-done(((f32[16,8,128]{2,1,0:T(8,128)}), f32[16,8,128]{2,1,0:T(8,128)S(1)}, u32[]{:S(2)}, u32[]{:S(2)}) %all-to-all-start.2) | async-done | bytes 65568 | tf_op jit(solution)/shard_map/all_to_all | solution.py:545
  118.0 0.6 copy.13
  118.5 0.0 collective-permute-done.in_ref
  118.5 2.3 %first.1.buffer_ref = bf16[512,2048]{1,0:T(8,128)(2,1)} custom-call(bf16[512,1024]{1,0:T(8,128)(2,1)} %collective-permute-done.in_ref), custom_call_target="tpu_custom_call" | custom-call | flops 1000000 | bytes 2097152 | tf_op jit(solution)/shard_map/first/pallas_call | solution.py:552
  120.8 2.9 %last.1 = (bf16[512,2048]{1,0:T(8,128)(2,1)}, f32[128,2048]{1,0:T(8,128)}) custom-call(s32[1]{0:T(128)} %bitcast.me_ref, bf16[512,2048]{1,0:T(8,128)(2,1)} %first.1.buffer_ref, bf16[512,1024]{1,0:T(8,128)(2,1)} %collective-permute-done.1.up_ref, bf16[128,512]{1,0:T(8,128)(2,1)} %get-tuple-element.102.refs_0_, ...), custom_call_target="tpu_custom_call", output_to_operand_aliasing={{0}: (1, {})} | custom-call | tf_op jit(solution)/shard_map/last/pallas_call | solution.py:563
  (7 shorter events, 0.0 us)
Async XLA Ops:
  10.1 9.3 %copy-start = (f32[1,32]{1,0:T(1,128)S(1)}, f32[1,32]{1,0:T(1,128)}, u32[]{:S(2)}) copy-start(f32[1,32]{1,0:T(1,128)} %param.14) | copy-start | bytes 388
  10.2 36.4 %all-to-all-start = ((bf16[16,264,128]{2,1,0:T(8,128)(2,1)}), bf16[16,264,128]{2,1,0:T(8,128)(2,1)}, u32[]{:S(2)}, u32[]{:S(2)}) async-start(bf16[16,264,128]{2,1,0:T(8,128)(2,1)} %get-tuple-element.57.pay_ref), calls=%async_computation | async-start | bytes 2162688 | tf_op jit(solution)/shard_map/all_to_all | solution.py:518
  48.7 31.8 %all-to-all-start.1 = ((bf16[16,256,128]{2,1,0:T(8,128)(2,1)}), bf16[16,256,128]{2,1,0:T(8,128)(2,1)}, u32[]{:S(2)}, u32[]{:S(2)}) async-start(bf16[16,256,128]{2,1,0:T(8,128)(2,1)} %scan.1), calls=%async_computation.1 | async-start | bytes 2097152 | tf_op jit(solution)/shard_map/all_to_all | solution.py:534
  88.9 29.6 %collective-permute-start = (bf16[512,1024]{1,0:T(8,128)(2,1)}, bf16[512,1024]{1,0:T(8,128)(2,1)}, u32[]{:S(2)}, u32[]{:S(2)}) collective-permute-start(bf16[512,1024]{1,0:T(8,128)(2,1)} %get-tuple-element.91), channel_id=1, source_target_pairs={{64,0},{128,64},{192,128},{65,1},{129,65},{193,129},{66,2},{130,66... | collective-permute-start | bytes 3145736 | tf_op jit(solution)/shard_map/ppermute | solution.py:543
  99.6 21.2 %collective-permute-start.1 = (bf16[512,1024]{1,0:T(8,128)(2,1)}, bf16[512,1024]{1,0:T(8,128)(2,1)}, u32[]{:S(2)}, u32[]{:S(2)}) collective-permute-start(bf16[512,1024]{1,0:T(8,128)(2,1)} %get-tuple-element.101), channel_id=1, source_target_pairs={{64,0},{128,64},{192,128},{65,1},{129,65},{193,129},{66,2},{130,66... | collective-permute-start | bytes 3145736 | tf_op jit(solution)/shard_map/ppermute | solution.py:543
  102.2 15.7 %all-to-all-start.2 = ((f32[16,8,128]{2,1,0:T(8,128)}), f32[16,8,128]{2,1,0:T(8,128)S(1)}, u32[]{:S(2)}, u32[]{:S(2)}) async-start(f32[16,8,128]{2,1,0:T(8,128)} %get-tuple-element.109), calls=%async_computation.2 | async-start | bytes 131072 | tf_op jit(solution)/shard_map/all_to_all | solution.py:545
  108.1 12.7 %collective-permute-start.2 = (bf16[128,512]{1,0:T(8,128)(2,1)}, bf16[128,512]{1,0:T(8,128)(2,1)}, u32[]{:S(2)}, u32[]{:S(2)}) collective-permute-start(bf16[128,512]{1,0:T(8,128)(2,1)} %get-tuple-element.103), channel_id=1, source_target_pairs={{0,1},{1,2},{2,3},{3,0},{4,5},{5,6},{6,7},{7,4},{8,9},{9,10},{10,1... | collective-permute-start | bytes 393224 | tf_op jit(solution)/shard_map/ppermute | solution.py:548
  109.6 11.2 %collective-permute-start.3 = (bf16[128,512]{1,0:T(8,128)(2,1)}, bf16[128,512]{1,0:T(8,128)(2,1)}, u32[]{:S(2)}, u32[]{:S(2)}) collective-permute-start(bf16[128,512]{1,0:T(8,128)(2,1)} %get-tuple-element.104), channel_id=1, source_target_pairs={{0,2},{1,3},{2,0},{3,1},{4,6},{5,7},{6,4},{7,5},{8,10},{9,11},{10,... | collective-permute-start | bytes 393224 | tf_op jit(solution)/shard_map/ppermute | solution.py:548
  110.7 10.1 %collective-permute-start.4 = (bf16[128,512]{1,0:T(8,128)(2,1)}, bf16[128,512]{1,0:T(8,128)(2,1)}, u32[]{:S(2)}, u32[]{:S(2)}) collective-permute-start(bf16[128,512]{1,0:T(8,128)(2,1)} %get-tuple-element.105), channel_id=1, source_target_pairs={{0,3},{1,0},{2,1},{3,2},{4,7},{5,4},{6,5},{7,6},{8,11},{9,8},{10,9... | collective-permute-start | bytes 393224 | tf_op jit(solution)/shard_map/ppermute | solution.py:548

commit v4 on v3

--- a/solution.py
+++ b/solution.py
@@ -15,6 +15,7 @@
 F32 = jnp.float32
 BF16 = jnp.bfloat16
 TAIL = 8
+WIDE = 1024
 
 
 def iota(shape, dim):
@@ -122,11 +123,11 @@
         wt_ref[...] = w_ref[...].astype(F32).T.astype(BF16)
         rt_ref[...] = r_ref[...].astype(F32).T.astype(BF16)
 
-    cl, ll = expand(cs_ref[...], base_ref, quad * (2 * LANES // HEADDIM))
+    cl, ll = expand(cs_ref[...], base_ref, quad * (WIDE // HEADDIM))
     before = running(row_ends(cl, chunks))
     total = before[chunks]
-    state = jnp.zeros((STATE, 2 * LANES), F32)
-    grad = jnp.zeros((STATE, 2 * LANES), F32)
+    state = jnp.zeros((STATE, WIDE), F32)
+    grad = jnp.zeros((STATE, WIDE), F32)
     for c in range(chunks):
         rows = chunk_rows(c)
         drawn = x_ref[rows].astype(F32) * jnp.exp((total - before[c]) - ll[rows])
@@ -136,10 +137,10 @@
         grad += mm(jnp.concatenate([r_t, r_t], 1), jnp.concatenate(split2(pushed), 0))
     carry = jnp.exp(total)
     carry_hi = carry.astype(BF16).astype(F32)
-    picked = jnp.where(iota((TAIL, 2 * LANES), 0) == 0, carry_hi, carry - carry_hi).astype(BF16)
+    picked = jnp.where(iota((TAIL, WIDE), 0) == 0, carry_hi, carry - carry_hi).astype(BF16)
     state_hi, state_lo = split2(state)
     grad = grad.astype(BF16)
-    for k in range(2):
+    for k in range(WIDE // LANES):
         lanes = slice(k * LANES, (k + 1) * LANES)
         pay_ref[k, :STATE] = state_hi[:, lanes]
         pay_ref[k, STATE : 2 * STATE] = grad[:, lanes]
@@ -398,9 +399,9 @@
     x, dy = mixer_input[0], output_grad[0]
     w, r, delta = write_vectors[0], read_vectors[0], delta_raw[0].T
 
-    steps = pairs // 2
+    steps = width // WIDE
     steps_per_group = steps // groups
-    col = pl.BlockSpec((length, 2 * LANES), lambda j: (0, j))
+    col = pl.BlockSpec((length, WIDE), lambda j: (0, j))
     grp = pl.BlockSpec((length, STATE), lambda j: (0, j // steps_per_group))
     grp_t = pl.BlockSpec((STATE, length), lambda j: (j // steps_per_group, 0))
     pay_rows = 2 * STATE + TAIL
@@ -409,8 +410,8 @@
         grid=(steps,),
         in_specs=[col, col, grp, grp, whole(heads, length), whole(1, heads), whole(1, heads)],
         out_specs=[
-            pl.BlockSpec((2, pay_rows, LANES), lambda j: (j, 0, 0)),
-            pl.BlockSpec((2, STATE, LANES), lambda j: (j, 0, 0)),
+            pl.BlockSpec((WIDE // LANES, pay_rows, LANES), lambda j: (j, 0, 0)),
+            pl.BlockSpec((WIDE // LANES, STATE, LANES), lambda j: (j, 0, 0)),
             whole(length, depth),
             whole(length // CHUNK, 2 * heads, CHUNK),
             grp_t,
@@ -424,7 +425,7 @@
             sds((groups * STATE, length), BF16),
             sds((groups * STATE, length), BF16),
         ],
-        scratch_shapes=[pltpu.VMEM((depth, 4 * LANES), jnp.int32)],
+        scratch_shapes=[pltpu.VMEM((depth, 2 * WIDE), jnp.int32)],
         compiler_params=params(),
         name="prep",
     )(x, dy, w, r, delta, log_rates, delta_bias)

time: 125 us -> 122 us (0.976)
  Pallas kernels: 64.6 us -> 62.2 us
    pallas_call x1, Pallas kernels: 9.51 us -> 7.11 us  [shards(): pl.pallas_call(functools.partial(prep_kernel, steps_per_group=steps_per_g...]
where the time goes in v4:
time: 122 us; the launch traced here: 121 us
  Pallas kernels  62.2 us (51%)
  starting transfers between devices  29.8 us (24%)
  waiting for transfers between devices  27.3 us (22%)
  local copies, waits for them, and re-layouts  1.33 us (1%)
    pallas_call x2, Pallas kernels, local(): pl.pallas_call(functools.partial(local_kernel, first_pair=first, heads=he...  30.6 us
    pallas_call x2, Pallas kernels, inter(): pl.pallas_call(functools.partial(inter_kernel, first_pair=first, heads=he...  17.2 us
    all_to_all x1, waiting for transfers between devices, shards(): lax.all_to_all(scanned, 'ctx', split_axis=0, concat_axis=0, tiled=True)  11.2 us
    all_to_all x1, waiting for transfers between devices, shards(): lax.all_to_all(pay, 'ctx', split_axis=0, concat_axis=0, tiled=True)  11 us
    all_to_all x1, starting transfers between devices, shards(): lax.all_to_all(pay, 'ctx', split_axis=0, concat_axis=0, tiled=True)  9.32 us
    pallas_call x1, Pallas kernels, shards(): pl.pallas_call(functools.partial(prep_kernel, steps_per_group=steps_per_g...  7.11 us
    all_to_all x1, starting transfers between devices, shards(): lax.all_to_all(sums, 'ctx', split_axis=0, concat_axis=0, tiled=True)  5.88 us
    all_to_all x1, starting transfers between devices, shards(): lax.all_to_all(scanned, 'ctx', split_axis=0, concat_axis=0, tiled=True)  5.24 us
  transfers between devices with their start and end apart: 8, of which 3 were waited for; matrix products, arithmetic and copies ran while one was open for 1% of the time, Pallas kernels for 34%

profile of v4, /device:TPU:50, one launch (start us, length us, event | category | flops | bytes accessed | tf_op | source)
XLA Modules:
  0.0 121.3 jit_solution(7494902366819010389)
XLA Ops:
  0.6 7.1 %prep.1 = (bf16[16,264,128]{2,1,0:T(8,128)(2,1)}, bf16[16,128,128]{2,1,0:T(8,128)(2,1)}, bf16[512,192]{1,0:T(8,128)(2,1)}, f32[4,64,128]{2,1,0:T(8,128)}, bf16[2...) custom-call(bf16[512,2048]{1,0:T(8,128)(2,1)} %bitcast.20, bf16[512,2048]{1,0:T(8,128)(2,1)} %bitcast.17, ...), custom_call_target="tpu_custom_call" | custom-call | tf_op jit(solution)/shard_map/prep/pallas_call | solution.py:408
  7.7 0.0 copy-start
  7.8 9.3 %all-to-all-start = ((bf16[16,264,128]{2,1,0:T(8,128)(2,1)}), bf16[16,264,128]{2,1,0:T(8,128)(2,1)}, u32[]{:S(2)}, u32[]{:S(2)}) async-start(bf16[16,264,128]{2,1,0:T(8,128)(2,1)} %get-tuple-element.57.pay_ref), calls=%async_computation | async-start | bytes 2162688 | tf_op jit(solution)/shard_map/all_to_all | solution.py:519
  17.1 0.1 broadcast_in_dim.21
  17.2 0.7 broadcast_in_dim.22.skip_ref
  17.8 15.3 %local.2 = (f32[8,512,128]{2,1,0:T(8,128)}, f32[512,128]{1,0:T(8,128)}, f32[512,256]{1,0:T(8,128)}, f32[8,128]{1,0:T(8,128)}, bf16[8,512,256]{2,1,0:T(8,128)(2,1)}, /*index=5*/f32[8,512,128]{2,1,0:T(8,128)}) custom-call(bf16[512,2048]{1,0:T(8,128)(2,1)} %bitcast.21, bf16[512,2048]{1,0:T(8,128)(2,1)} %bitcast.18, bf16[512,256]{1,0:T(8,128)(2,1)} %bitcast.26, ...), custom_call_target="tpu_custom_call" | custom-call | flops 20000000000 | bytes 67108864 | tf_op jit(solution)/shard_map/local/pallas_call | solution.py:457
  33.1 11.0 %all-to-all-done.in_ref.mark_ref = bf16[16,264,128]{2,1,0:T(8,128)(2,1)} async-done(((bf16[16,264,128]{2,1,0:T(8,128)(2,1)}), bf16[16,264,128]{2,1,0:T(8,128)(2,1)}, u32[]{:S(2)}, u32[]{:S(2)}) %all-to-all-start) | async-done | bytes 1081376 | tf_op jit(solution)/shard_map/all_to_all | solution.py:519
  44.1 2.1 %scan.1 = bf16[16,256,128]{2,1,0:T(8,128)(2,1)} custom-call(bf16[16,264,128]{2,1,0:T(8,128)(2,1)} %all-to-all-done.in_ref.mark_ref, bf16[16,264,128]{2,1,0:T(8,128)(2,1)} %all-to-all-done.in_ref.mark_ref), custom_call_target="tpu_custom_call" | custom-call | tf_op jit(solution)/shard_map/scan/pallas_call | solution.py:522
  46.3 5.2 %all-to-all-start.1 = ((bf16[16,256,128]{2,1,0:T(8,128)(2,1)}), bf16[16,256,128]{2,1,0:T(8,128)(2,1)}, u32[]{:S(2)}, u32[]{:S(2)}) async-start(bf16[16,256,128]{2,1,0:T(8,128)(2,1)} %scan.1), calls=%async_computation.1 | async-start | bytes 2097152 | tf_op jit(solution)/shard_map/all_to_all | solution.py:535
  51.5 15.3 %local.3 = (f32[8,512,128]{2,1,0:T(8,128)}, f32[512,128]{1,0:T(8,128)}, f32[512,256]{1,0:T(8,128)}, f32[8,128]{1,0:T(8,128)}, bf16[8,512,256]{2,1,0:T(8,128)(2,1)}, /*index=5*/f32[8,512,128]{2,1,0:T(8,128)}) custom-call(bf16[512,2048]{1,0:T(8,128)(2,1)} %bitcast.22, bf16[512,2048]{1,0:T(8,128)(2,1)} %bitcast.19, bf16[512,256]{1,0:T(8,128)(2,1)} %bitcast.27, ...), custom_call_target="tpu_custom_call" | custom-call | flops 20000000000 | bytes 67108864 | tf_op jit(solution)/shard_map/local/pallas_call | solution.py:457
  66.8 11.2 %all-to-all-done.1.st_ref = bf16[16,256,128]{2,1,0:T(8,128)(2,1)} async-done(((bf16[16,256,128]{2,1,0:T(8,128)(2,1)}), bf16[16,256,128]{2,1,0:T(8,128)(2,1)}, u32[]{:S(2)}, u32[]{:S(2)}) %all-to-all-start.1) | async-done | bytes 1048608 | tf_op jit(solution)/shard_map/all_to_all | solution.py:535
  78.0 8.5 %inter.2 = (bf16[512,1024]{1,0:T(8,128)(2,1)}, f32[32,512]{1,0:T(8,128)}, f32[1,8,128]{2,1,0:T(8,128)}, bf16[512,256]{1,0:T(8,128)(2,1)}) custom-call(s32[1]{0:T(128)} %bitcast.me_ref, bf16[8,512,256]{2,1,0:T(8,128)(2,1)} %get-tuple-element.83.pushed_ref, f32[8,512,128]{2,1,0:T(8,128)} %get-tuple-element.84.tail_ref, bf16[512,2048]{1,0:T(8,128)(2,1)} %bitcast.23, ...), custom_call_target="tpu_custom_call" | custom-call | flops 4000000000 | bytes 16777216 | tf_op jit(solution)/shard_map/inter/pallas_call | solution.py:490
  86.5 1.9 %collective-permute-start = (bf16[512,1024]{1,0:T(8,128)(2,1)}, bf16[512,1024]{1,0:T(8,128)(2,1)}, u32[]{:S(2)}, u32[]{:S(2)}) collective-permute-start(bf16[512,1024]{1,0:T(8,128)(2,1)} %get-tuple-element.91), channel_id=1, source_target_pairs={{64,0},{128,64},{192,128},{65,1},{129,65},{193,129},{66,2},{130,66... | collective-permute-start | bytes 3145736 | tf_op jit(solution)/shard_map/ppermute | solution.py:544
  88.5 8.7 %inter.3 = (bf16[512,1024]{1,0:T(8,128)(2,1)}, f32[32,512]{1,0:T(8,128)}, f32[16,8,128]{2,1,0:T(8,128)}, bf16[128,512]{1,0:T(8,128)(2,1)}, bf16[128,512]{1,0:T(8...) custom-call(s32[1]{0:T(128)} %bitcast.me_ref, bf16[8,512,256]{2,1,0:T(8,128)(2,1)} %get-tuple-element.92.pushed_ref, ...), custom_call_target="tpu_custom_call" | custom-call | flops 4000000000 | bytes 16777216 | tf_op jit(solution)/shard_map/inter/pallas_call | solution.py:490
  97.2 2.6 %collective-permute-start.1 = (bf16[512,1024]{1,0:T(8,128)(2,1)}, bf16[512,1024]{1,0:T(8,128)(2,1)}, u32[]{:S(2)}, u32[]{:S(2)}) collective-permute-start(bf16[512,1024]{1,0:T(8,128)(2,1)} %get-tuple-element.101), channel_id=1, source_target_pairs={{64,0},{128,64},{192,128},{65,1},{129,65},{193,129},{66,2},{130,66... | collective-permute-start | bytes 3145736 | tf_op jit(solution)/shard_map/ppermute | solution.py:544
  99.8 5.9 %all-to-all-start.2 = ((f32[16,8,128]{2,1,0:T(8,128)}), f32[16,8,128]{2,1,0:T(8,128)S(1)}, u32[]{:S(2)}, u32[]{:S(2)}) async-start(f32[16,8,128]{2,1,0:T(8,128)} %get-tuple-element.109), calls=%async_computation.2 | async-start | bytes 131072 | tf_op jit(solution)/shard_map/all_to_all | solution.py:546
  105.7 1.5 %collective-permute-start.2 = (bf16[128,512]{1,0:T(8,128)(2,1)}, bf16[128,512]{1,0:T(8,128)(2,1)}, u32[]{:S(2)}, u32[]{:S(2)}) collective-permute-start(bf16[128,512]{1,0:T(8,128)(2,1)} %get-tuple-element.103), channel_id=1, source_target_pairs={{0,1},{1,2},{2,3},{3,0},{4,5},{5,6},{6,7},{7,4},{8,9},{9,10},{10,1... | collective-permute-start | bytes 393224 | tf_op jit(solution)/shard_map/ppermute | solution.py:549
  107.2 1.1 collective-permute-start.3
  108.3 2.2 %collective-permute-start.4 = (bf16[128,512]{1,0:T(8,128)(2,1)}, bf16[128,512]{1,0:T(8,128)(2,1)}, u32[]{:S(2)}, u32[]{:S(2)}) collective-permute-start(bf16[128,512]{1,0:T(8,128)(2,1)} %get-tuple-element.105), channel_id=1, source_target_pairs={{0,3},{1,0},{2,1},{3,2},{4,7},{5,4},{6,5},{7,6},{8,11},{9,8},{10,9... | collective-permute-start | bytes 393224 | tf_op jit(solution)/shard_map/ppermute | solution.py:549
  110.5 5.0 %all-to-all-done.2 = f32[16,8,128]{2,1,0:T(8,128)S(1)} async-done(((f32[16,8,128]{2,1,0:T(8,128)}), f32[16,8,128]{2,1,0:T(8,128)S(1)}, u32[]{:S(2)}, u32[]{:S(2)}) %all-to-all-start.2) | async-done | bytes 65568 | tf_op jit(solution)/shard_map/all_to_all | solution.py:546
  115.6 0.6 copy.13
  116.1 2.3 %first.1.buffer_ref = bf16[512,2048]{1,0:T(8,128)(2,1)} custom-call(bf16[512,1024]{1,0:T(8,128)(2,1)} %collective-permute-done.in_ref), custom_call_target="tpu_custom_call" | custom-call | flops 1000000 | bytes 2097152 | tf_op jit(solution)/shard_map/first/pallas_call | solution.py:553
  118.4 0.0 collective-permute-done.2.refs_1_
  118.4 2.9 %last.1 = (bf16[512,2048]{1,0:T(8,128)(2,1)}, f32[128,2048]{1,0:T(8,128)}) custom-call(s32[1]{0:T(128)} %bitcast.me_ref, bf16[512,2048]{1,0:T(8,128)(2,1)} %first.1.buffer_ref, bf16[512,1024]{1,0:T(8,128)(2,1)} %collective-permute-done.1.up_ref, bf16[128,512]{1,0:T(8,128)(2,1)} %get-tuple-element.102.refs_0_, ...), custom_call_target="tpu_custom_call", output_to_operand_aliasing={{0}: (1, {})} | custom-call | tf_op jit(solution)/shard_map/last/pallas_call | solution.py:564
  (7 shorter events, 0.0 us)
Async XLA Ops:
  7.7 9.3 %copy-start = (f32[1,32]{1,0:T(1,128)S(1)}, f32[1,32]{1,0:T(1,128)}, u32[]{:S(2)}) copy-start(f32[1,32]{1,0:T(1,128)} %param.14) | copy-start | bytes 388
  7.8 36.4 %all-to-all-start = ((bf16[16,264,128]{2,1,0:T(8,128)(2,1)}), bf16[16,264,128]{2,1,0:T(8,128)(2,1)}, u32[]{:S(2)}, u32[]{:S(2)}) async-start(bf16[16,264,128]{2,1,0:T(8,128)(2,1)} %get-tuple-element.57.pay_ref), calls=%async_computation | async-start | bytes 2162688 | tf_op jit(solution)/shard_map/all_to_all | solution.py:519
  46.3 31.8 %all-to-all-start.1 = ((bf16[16,256,128]{2,1,0:T(8,128)(2,1)}), bf16[16,256,128]{2,1,0:T(8,128)(2,1)}, u32[]{:S(2)}, u32[]{:S(2)}) async-start(bf16[16,256,128]{2,1,0:T(8,128)(2,1)} %scan.1), calls=%async_computation.1 | async-start | bytes 2097152 | tf_op jit(solution)/shard_map/all_to_all | solution.py:535
  86.5 29.6 %collective-permute-start = (bf16[512,1024]{1,0:T(8,128)(2,1)}, bf16[512,1024]{1,0:T(8,128)(2,1)}, u32[]{:S(2)}, u32[]{:S(2)}) collective-permute-start(bf16[512,1024]{1,0:T(8,128)(2,1)} %get-tuple-element.91), channel_id=1, source_target_pairs={{64,0},{128,64},{192,128},{65,1},{129,65},{193,129},{66,2},{130,66... | collective-permute-start | bytes 3145736 | tf_op jit(solution)/shard_map/ppermute | solution.py:544
  97.2 21.2 %collective-permute-start.1 = (bf16[512,1024]{1,0:T(8,128)(2,1)}, bf16[512,1024]{1,0:T(8,128)(2,1)}, u32[]{:S(2)}, u32[]{:S(2)}) collective-permute-start(bf16[512,1024]{1,0:T(8,128)(2,1)} %get-tuple-element.101), channel_id=1, source_target_pairs={{64,0},{128,64},{192,128},{65,1},{129,65},{193,129},{66,2},{130,66... | collective-permute-start | bytes 3145736 | tf_op jit(solution)/shard_map/ppermute | solution.py:544
  99.8 15.7 %all-to-all-start.2 = ((f32[16,8,128]{2,1,0:T(8,128)}), f32[16,8,128]{2,1,0:T(8,128)S(1)}, u32[]{:S(2)}, u32[]{:S(2)}) async-start(f32[16,8,128]{2,1,0:T(8,128)} %get-tuple-element.109), calls=%async_computation.2 | async-start | bytes 131072 | tf_op jit(solution)/shard_map/all_to_all | solution.py:546
  105.7 12.7 %collective-permute-start.2 = (bf16[128,512]{1,0:T(8,128)(2,1)}, bf16[128,512]{1,0:T(8,128)(2,1)}, u32[]{:S(2)}, u32[]{:S(2)}) collective-permute-start(bf16[128,512]{1,0:T(8,128)(2,1)} %get-tuple-element.103), channel_id=1, source_target_pairs={{0,1},{1,2},{2,3},{3,0},{4,5},{5,6},{6,7},{7,4},{8,9},{9,10},{10,1... | collective-permute-start | bytes 393224 | tf_op jit(solution)/shard_map/ppermute | solution.py:549
  107.2 11.2 %collective-permute-start.3 = (bf16[128,512]{1,0:T(8,128)(2,1)}, bf16[128,512]{1,0:T(8,128)(2,1)}, u32[]{:S(2)}, u32[]{:S(2)}) collective-permute-start(bf16[128,512]{1,0:T(8,128)(2,1)} %get-tuple-element.104), channel_id=1, source_target_pairs={{0,2},{1,3},{2,0},{3,1},{4,6},{5,7},{6,4},{7,5},{8,10},{9,11},{10,... | collective-permute-start | bytes 393224 | tf_op jit(solution)/shard_map/ppermute | solution.py:549
  108.3 10.1 %collective-permute-start.4 = (bf16[128,512]{1,0:T(8,128)(2,1)}, bf16[128,512]{1,0:T(8,128)(2,1)}, u32[]{:S(2)}, u32[]{:S(2)}) collective-permute-start(bf16[128,512]{1,0:T(8,128)(2,1)} %get-tuple-element.105), channel_id=1, source_target_pairs={{0,3},{1,0},{2,1},{3,2},{4,7},{5,4},{6,5},{7,6},{8,11},{9,8},{10,9... | collective-permute-start | bytes 393224 | tf_op jit(solution)/shard_map/ppermute | solution.py:549
